TPU v7x, 768 devices: a whole 4x8x12 slice. The times are simulated.
768 devices in a mesh: fsdp: 24 (over z_hi, x, core), ctx: 32 (over z_lo, y).
Axes of the slice: x: 4, y: 8, z: 12 (z_hi: 3, z_lo: 4; z = z_hi * 4 + z_lo), core: 2. Of those that a mesh axis runs over, the one named last changes fastest.
Arguments:
- frames: bfloat16 [24, 16384, 1536], P('fsdp', 'ctx'), may hold values from -120 to 120
- lengths: int32 [24], P('fsdp'), may hold values from 4096 to 16384, as said below
- ln_gain: float32 [1536], replicated, may hold values from 0.1 to 1.9
- w_in: bfloat16 [1536, 1536], P('fsdp'), may hold values from -0.15625 to 0.15625
- dw_kernel: float32 [31, 768], replicated, may hold values from -1 to 1
- bn_gain: float32 [768], replicated, may hold values from 0.1 to 1.9
- bn_shift: float32 [768], replicated, may hold values from -3 to 3
- w_out: bfloat16 [768, 1536], P('fsdp'), may hold values from -0.21875 to 0.21875
Outputs:
- result: bfloat16 [24, 16384, 1536], P('fsdp', 'ctx')
Inputs may be any that keep to these rules, and one draw needn't show every extreme that they name: frames 0 to lengths[r] - 1 of recording r are valid; one recording is full and one has exactly 4096 valid frames.
All inputs are finite; a program needn't handle non-finite values.
Results may differ from a plain program's by a relative error of at most 0.0076.
Values may be sent and summed in bfloat16 or wider, within the bound.
A program may use at most 32 MiB of HBM per device.

v0:
```python
import jax
import jax.numpy as jnp
from jax import lax
from jax.sharding import PartitionSpec as P


def extended(cells, sides, width):
    for axis, dim in sides:
        count = lax.axis_size(axis)
        ends = count - 1
        head = lax.slice_in_dim(cells, 0, width, axis=dim)
        tail = lax.slice_in_dim(cells, cells.shape[dim] - width, cells.shape[dim], axis=dim)
        cells = jnp.concatenate(
            [
                lax.ppermute(tail, axis, [(i, (i + 1) % count) for i in range(ends)]),
                cells,
                lax.ppermute(head, axis, [((i + 1) % count, i) for i in range(ends)]),
            ],
            axis=dim,
        )
    return cells


def normalize_rows(rows_in, ln_gain):
    values = rows_in.astype(jnp.float32)
    centre = jnp.mean(values, axis=-1, keepdims=True)
    deviate = values - centre
    spread = jnp.mean(deviate * deviate, axis=-1, keepdims=True)
    return (deviate * lax.rsqrt(spread + 1e-05) * ln_gain).astype(jnp.bfloat16)


def body(frames, lengths, ln_gain, w_in, dw_kernel, bn_gain, bn_shift, w_out):
    rec_count, row_count, model_width = frames.shape
    kernel_taps, channels = dw_kernel.shape
    half_width = (kernel_taps - 1) // 2
    flat_frames = frames.reshape(rec_count * row_count, model_width)
    normed = normalize_rows(flat_frames, ln_gain)
    position = lax.axis_index("ctx") * row_count + jnp.arange(row_count, dtype=jnp.int32)
    valid_rows = (position[None, :] < lengths[:, None]).reshape(rec_count * row_count, 1)
    columns = normed
    projected = jnp.dot(
        columns,
        lax.all_gather(w_in, "fsdp", axis=0, tiled=True),
        preferred_element_type=jnp.float32,
    )
    gated = jnp.where(
        valid_rows, projected[:, :channels] * jax.nn.sigmoid(projected[:, channels:]), 0.0
    )
    gated = gated.astype(jnp.bfloat16).reshape(rec_count, row_count, channels)
    padded = extended(gated, (("ctx", 1),), half_width).astype(jnp.float32)
    convolved = jnp.zeros((rec_count, row_count, channels), jnp.float32)
    for tap_index in range(kernel_taps):
        convolved = convolved + padded[:, tap_index : tap_index + row_count] * dw_kernel[tap_index]
    valid_mask = valid_rows.reshape(rec_count, row_count, 1).astype(jnp.float32)
    local_count = jnp.sum(valid_mask)
    masked_conv = convolved * valid_mask
    chan_total, valid_count = lax.psum(
        (jnp.sum(masked_conv, axis=(0, 1)), local_count), ("fsdp", "ctx")
    )
    chan_mean = chan_total / valid_count
    centered = (convolved - chan_mean) * valid_mask
    chan_square = lax.psum(jnp.sum(centered * centered, axis=(0, 1)), ("fsdp", "ctx"))
    chan_var = chan_square / valid_count
    scaled = (convolved - chan_mean) * lax.rsqrt(chan_var + 1e-05) * bn_gain + bn_shift
    activated = jax.nn.silu(scaled).astype(jnp.bfloat16).reshape(rec_count * row_count, channels)
    columns = activated
    result_rows = jnp.dot(
        columns,
        lax.all_gather(w_out, "fsdp", axis=0, tiled=True),
        preferred_element_type=jnp.float32,
    )
    result_rows = jnp.where(valid_rows, result_rows, 0.0).astype(jnp.bfloat16)
    return result_rows.reshape(rec_count, row_count, model_width)


def solution(mesh):
    return jax.shard_map(
        body,
        mesh=mesh,
        in_specs=(
            P("fsdp", "ctx", None),
            P("fsdp"),
            P(),
            P("fsdp", None),
            P(),
            P(),
            P(),
            P("fsdp", None),
        ),
        out_specs=P("fsdp", "ctx", None),
        check_vma=False,
    )
```

profile of v0, /device:TPU:1, one launch (start us, length us, event | category | flops | bytes accessed | tf_op | source)
XLA Modules:
  0.0 371.9 jit_solution(11662310362302897012)
XLA Ops:
  6.5 0.0 copy-start
  6.5 0.0 all-gather.3.cloned.1.call-start
  6.5 0.7 all-gather.3.cloned.1.call-update
  7.3 0.0 all-gather.5.cloned.1.call-start
  7.3 0.7 all-gather.5.cloned.1.call-update
  8.7 0.0 copy-start.1
  8.7 0.0 copy-start.2
  8.7 1.7 convert_reduce_fusion
  10.4 0.0 copy-done
  10.4 0.5 fusion.3
  11.0 0.0 copy-done.1
  11.0 0.2 slice_reduce_fusion.30
  11.2 0.6 convert_reduce_fusion.1
  11.8 100.9 %all-gather.3.cloned.1.call-done = bf16[1536,1536]{1,0:T(8,128)(2,1)} async-done(((bf16[64,1536]{1,0:T(8,128)(2,1)}), bf16[1536,1536]{1,0:T(8,128)(2,1)}) %all-gather.3.cloned.1.call-update) | async-done | bytes 4718608 | tf_op jit(solution)/shard_map/all_gather | solution.py:43
  112.6 0.0 copy-done.2
  112.7 4.7 %fusion.8 = f32[512,1536]{1,0:T(8,128)S(1)} fusion(bf16[1536,1536]{1,0:T(8,128)(2,1)} %all-gather.3.cloned.1.call-done, bf16[1,512,1536]{2,1,0:T(8,128)(2,1)S(1)} %copy-done, f32[1536]{0:T(1024)S(1)} %copy-done.2, f32[512]{0:T(512)S(1)} %add_rsqrt_fusion.1, f32[512]{0:T(512)S(1)} %broadcast_multiply_fusion), kind=kOutput, calls=%fused_computation.11 | convolution fusion | flops 2419851264 | bytes 9447424 | tf_op jit(solution)/shard_map/dot_general | solution.py:41
  117.3 0.4 fusion.54
  117.8 3.1 collective-permute-start
  120.9 1.3 collective-permute-start.1
  122.2 0.1 slice_reduce_fusion.29
  122.3 0.0 collective-permute-done
  122.3 3.1 collective-permute-done.1
  125.5 0.2 maximum_convert_fusion
  125.6 6.6 %multiply_reduce_fusion.1 = (f32[768]{0:T(1024)S(1)}, f32[1,512,768]{2,1,0:T(8,128)S(1)}) fusion(f32[512]{0:T(512)S(1)} %convert_element_type.43, f32[768]{0:T(1024)S(1)} %get-tuple-element.34, f32[1,542,768]{2,1,0:T(8,128)S(1)} %maximum_convert_fusion, f32[768]{0:T(1024)S(1)} %get-tuple-element.35, f32[768]{0:T(1024)S(1)} %get-tuple-element.6, ...), kind=kLoop, calls=%fused_computation.81 | loop fusion | flops 24771840 | bytes 50432000 | tf_op jit(solution)/shard_map/reduce_sum | solution.py:58
  132.3 0.0 copy-start.3
  132.3 0.0 copy-start.4
  132.3 123.1 %all-reduce = (f32[768]{0:T(1024)S(1)}, f32[]{:T(128)}) all-reduce(f32[768]{0:T(1024)S(1)} %get-tuple-element.40, f32[]{:T(128)} %get-tuple-element.38), channel_id=1, replica_groups=mesh['fsdp'=24,'ctx'=32] {'fsdp','ctx'}, use_global_device_ids=true, to_apply=%region_3.4 | all-reduce | flops 769 | bytes 6152 | tf_op jit(solution)/shard_map/psum | solution.py:57
  255.4 0.6 broadcast_divide_fusion
  256.0 0.3 multiply_reduce_fusion
  256.3 103.7 %psum.23 = f32[768]{0:T(1024)S(1)} all-reduce(f32[768]{0:T(1024)S(1)} %multiply_reduce_fusion), channel_id=1, replica_groups=mesh['fsdp'=24,'ctx'=32] {'fsdp','ctx'}, use_global_device_ids=true, to_apply=%region_7.8 | all-reduce | flops 768 | bytes 6144 | tf_op jit(solution)/shard_map/psum | solution.py:62
  360.0 0.7 add_rsqrt_fusion
  360.7 0.0 all-gather.5.cloned.1.call-done
  360.7 0.0 copy-done.3
  360.7 0.0 copy-done.4
  360.7 4.4 %fusion.7 = bf16[1,512,1536]{2,1,0:T(8,128)(2,1)} fusion(bf16[768,1536]{1,0:T(8,128)(2,1)} %all-gather.5.cloned.1.call-done, pred[512]{0:T(512)(128)(4,1)S(1)} %get-tuple-element.39, f32[1,512,768]{2,1,0:T(8,128)S(1)} %get-tuple-element.41, f32[768]{0:T(1024)S(1)} %copy-done.3, f32[768]{0:T(1024)S(1)} %copy-done.4, f32[768]{0:T(1024)S(1)} %add_rsqrt_fusion, ...), kind=kOutput, calls=%fused_computation.10 | convolution fusion | flops 1213071360 | bytes 5517824 | tf_op jit(solution)/shard_map/dot_general | solution.py:67
  (4 shorter events, 0.0 us)
Async XLA Ops:
  6.5 3.9 %copy-start = (bf16[1,512,1536]{2,1,0:T(8,128)(2,1)S(1)}, bf16[1,512,1536]{2,1,0:T(8,128)(2,1)}, u32[]{:S(2)}) copy-start(bf16[1,512,1536]{2,1,0:T(8,128)(2,1)} %param.8) | copy-start | bytes 4718596
  6.5 106.1 %all-gather.3.cloned.1.call-start = ((), (), s32[]{:S(2)}) async-start(), calls=%async_computation | async-start | bytes 4915200 | tf_op jit(solution)/shard_map/all_gather | solution.py:43
  7.3 353.4 %all-gather.5.cloned.1.call-start = ((), (), s32[]{:S(2)}) async-start(), calls=%async_computation.1 | async-start | bytes 2457600 | tf_op jit(solution)/shard_map/all_gather | solution.py:69
  8.7 2.3 copy-start.1
  8.7 104.0 %copy-start.2 = (f32[1536]{0:T(1024)S(1)}, f32[1536]{0:T(1024)}, u32[]{:S(2)}) copy-start(f32[1536]{0:T(1024)} %param.10) | copy-start | bytes 18436
  117.8 4.5 %collective-permute-start = (bf16[1,15,768]{2,1,0:T(8,128)(2,1)S(1)}, bf16[1,15,768]{2,1,0:T(8,128)(2,1)S(1)}, u32[]{:S(2)}, u32[]{:S(2)}) collective-permute-start(bf16[1,15,768]{2,1,0:T(8,128)(2,1)S(1)} %get-tuple-element.42), channel_id=1, source_target_pairs={{0,1},{1,2},{2,3},{3,4},{4,5},{5,6},{6,7},{7,8},{8,9},{9,10},{10,1... | collective-permute-start | bytes 69128 | tf_op jit(solution)/shard_map/ppermute | solution.py:15
  120.9 4.6 %collective-permute-start.1 = (bf16[1,15,768]{2,1,0:T(8,128)(2,1)S(1)}, bf16[1,15,768]{2,1,0:T(8,128)(2,1)S(1)}, u32[]{:S(2)}, u32[]{:S(2)}) collective-permute-start(bf16[1,15,768]{2,1,0:T(8,128)(2,1)S(1)} %get-tuple-element.43), channel_id=1, source_target_pairs={{1,0},{2,1},{3,2},{4,3},{5,4},{6,5},{7,6},{8,7},{9,8},{10,9},{11,1... | collective-permute-start | bytes 69128 | tf_op jit(solution)/shard_map/ppermute | solution.py:17
  132.3 228.4 %copy-start.3 = (f32[768]{0:T(1024)S(1)}, f32[768]{0:T(1024)}, u32[]{:S(2)}) copy-start(f32[768]{0:T(1024)} %param.14) | copy-start | bytes 9220
  132.3 228.4 %copy-start.4 = (f32[768]{0:T(1024)S(1)}, f32[768]{0:T(1024)}, u32[]{:S(2)}) copy-start(f32[768]{0:T(1024)} %param.13) | copy-start | bytes 9220
Sparse Core Ops, SparseCore 0:
  11.4 101.2 all-gather.2
  116.7 84.5 all-gather.4
where the time goes:
time: 372 us
  blocking collectives  227 us (61%)
  waiting for transfers between devices  105 us (28%)
  between operations  14.2 us (4%)
  other arithmetic  11.7 us (3%)
  matrix products  9.03 us (2%)
  starting transfers between devices  4.44 us (1%)
    psum x1, blocking collectives, body(): lax.psum((jnp.sum(masked_conv, axis=(0, 1)), local_count), ('fsdp', 'ctx'))  123 us
    psum x1, blocking collectives, body(): lax.psum(jnp.sum(centered * centered, axis=(0, 1)), ('fsdp', 'ctx'))  104 us
    all_gather x1, waiting for transfers between devices, body(): lax.all_gather(w_in, 'fsdp', axis=0, tiled=True)  101 us
  transfers between devices with their start and end apart: 4, of which 2 were waited for; matrix products, arithmetic and copies ran while one was open for 4% of the time, Pallas kernels for 0%

commit v1 on v0

v1 whole, which is shorter than its diff:
```python
import jax
import jax.numpy as jnp
from jax import lax
from jax.experimental import pallas as pl
from jax.experimental.pallas import tpu as pltpu
from jax.sharding import PartitionSpec as P

MESH = pl.DeviceIdType.MESH
BF16 = jnp.bfloat16
F32 = jnp.float32
NX, NY, NZ = 4, 8, 12
ROWS, EDGE = 512, 16
ALL = ROWS + 2 * EDGE
TAPS, CH, D = 31, 768, 1536
STRIPS = CH // 128
LAYERS = 3
ZS, XS, YS, CS = 0, 2, 11, 17
SEMS = 23


def device_of(x, y, z, c):
    return (((z // 4) * NX + x) * 2 + c, (z % 4) * NY + y)


def sigmoid(v):
    return 0.5 * jnp.tanh(0.5 * v) + 0.5


def combine(all_ref, parts):
    means = [all_ref[i, 0:8, :] for i in range(parts)]
    counts = [all_ref[i, 6:7, :] for i in range(parts)]
    squares = [all_ref[i, 8:16, :] for i in range(parts)]
    total = sum(counts[1:], counts[0])
    inverse = 1.0 / jnp.maximum(total, 1.0)
    weighted = [m * n for m, n in zip(means, counts)]
    mean = sum(weighted[1:], weighted[0]) * inverse
    spread = sum(squares[1:], squares[0])
    for m, n in zip(means, counts):
        spread = spread + n * (m - mean) * (m - mean)
    row = lax.broadcasted_iota(jnp.int32, (8, 128), 0)
    mean = jnp.where(row == 6, jnp.broadcast_to(total, (8, 128)), mean)
    return mean, spread


def kernel(
    frames, lengths, ln_gain, w_in, dw, bn_gain, bn_shift, w_out, out,
    xbuf, nbuf, wbuf, vbuf, acc, gbuf, cbuf, act, r1, r2, r3, final,
    gsend, grecv, hsend, hrecv, ssend, srecv, lsem,
):
    f, t = lax.axis_index("fsdp"), lax.axis_index("ctx")
    x, c = (f // 2) % NX, f % 2
    y = t % NY
    zh, zl = f // (2 * NX), t // NY
    z = zh * 4 + zl
    par = y % 2
    up, down = (zh + 1) % 3, (zh + 2) % 3
    groups = (zh, up, down)

    def at(dx=0, dy=0, dz=0, dc=0):
        return device_of((x + dx) % NX, (y + dy) % NY, (z + dz) % NZ, (c + dc) % 2)

    left, right = (f, (t + 31) % 32), (f, (t + 1) % 32)
    slot1 = x * 2 + c

    def peer1(d):
        to = (slot1 + d) % 8
        return device_of(to // 2, y, z, to % 2)

    peers = [left, right]
    peers += [peer1(d) for d in range(1, 8)]
    peers += [at(dy=d) for d in range(1, NY)]
    peers += [at(dz=d) for d in range(1, NZ)]

    rows_of = [par * 32, par * 32 + 16, par * 16]
    other_of = [(1 - par) * 32, (1 - par) * 32 + 16, (1 - par) * 16]
    bufs = [wbuf, wbuf, vbuf]
    shards = [w_in, w_in, w_out]

    def span(start):
        return pl.ds(pl.multiple_of(start, 16), 16)

    own_frames = pltpu.make_async_copy(frames.at[0], xbuf.at[pl.ds(EDGE, ROWS)], lsem.at[0])
    own_frames.start()
    own_rows = []
    for layer in range(LAYERS):
        copy = pltpu.make_async_copy(
            shards[layer].at[span(rows_of[layer])],
            bufs[layer].at[zh, x, c, span(rows_of[layer])],
            lsem.at[1 + layer],
        )
        copy.start()
        own_rows.append(copy)

    barrier = pltpu.get_barrier_semaphore()
    for peer in peers:
        pl.semaphore_signal(barrier, inc=1, device_id=peer, device_id_type=MESH)
    pl.semaphore_wait(barrier, len(peers))

    sent = []

    def remote(src, dst, sems, k, to):
        return pltpu.make_async_remote_copy(
            src_ref=src, dst_ref=dst, send_sem=sems[0].at[k], recv_sem=sems[1].at[k],
            device_id=to, device_id_type=MESH,
        )

    def send(*args):
        copy = remote(*args)
        copy.start()
        sent.append(copy)

    def arrived(dst, sems, k):
        remote(dst, dst, sems, k, at(dc=1)).wait_recv()

    def gs(layer):
        return (gsend.at[layer], grecv.at[layer])

    XD = (1, 3, 2)

    def unit(layer, group, xs):
        return bufs[layer].at[group, xs, c, span(rows_of[layer])]

    def z_send(layer):
        src = shards[layer].at[span(rows_of[layer])]
        dst = unit(layer, zh, x)
        send(src, dst, gs(layer), ZS + 0, at(dz=-4))
        send(src, dst, gs(layer), ZS + 1, at(dz=4))

    def z_wait(layer):
        arrived(unit(layer, up, x), gs(layer), ZS + 0)
        arrived(unit(layer, down, x), gs(layer), ZS + 1)

    def x_send(layer, which):
        dst = unit(layer, groups[which], x)
        src = shards[layer].at[span(rows_of[layer])] if which == 0 else dst
        for i, d in enumerate(XD):
            send(src, dst, gs(layer), XS + which * 3 + i, at(dx=d))

    def x_wait(layer, which):
        for i, d in enumerate(XD):
            arrived(unit(layer, groups[which], (x + 4 - d) % NX), gs(layer), XS + which * 3 + i)

    def piece(layer, group, rows, side):
        return bufs[layer].at[group, :, c, span(rows), pl.ds(side * CH, CH)]

    def y_send(layer, which):
        for side, d in ((0, 1), (1, 7)):
            ref = piece(layer, groups[which], rows_of[layer], side)
            send(ref, ref, gs(layer), YS + which * 2 + side, at(dy=d))

    def y_wait(layer, which):
        for side in (0, 1):
            arrived(piece(layer, groups[which], other_of[layer], side), gs(layer), YS + which * 2 + side)

    def block(layer, group, core, rows):
        return bufs[layer].at[group, :, core, span(rows)]

    def c_send(layer, which, half):
        rows = (rows_of, other_of)[half][layer]
        ref = block(layer, groups[which], c, rows)
        send(ref, ref, gs(layer), CS + which * 2 + half, at(dc=1))

    def c_wait(layer, which):
        for half in (0, 1):
            rows = (rows_of, other_of)[half][layer]
            arrived(block(layer, groups[which], 1 - c, rows), gs(layer), CS + which * 2 + half)

    z_send(0)
    x_send(0, 0)
    z_send(1)
    x_send(1, 0)
    hs = (hsend, hrecv)
    send(frames.at[0, pl.ds(ROWS - EDGE, EDGE)], xbuf.at[pl.ds(0, EDGE)], hs, 0, right)
    send(frames.at[0, pl.ds(0, EDGE)], xbuf.at[pl.ds(EDGE + ROWS, EDGE)], hs, 1, left)

    def norm(start, size):
        values = xbuf[pl.ds(start, size), :].astype(F32)
        centre = jnp.mean(values, axis=-1, keepdims=True)
        deviate = values - centre
        spread = jnp.mean(deviate * deviate, axis=-1, keepdims=True)
        normed = (deviate * lax.rsqrt(spread + 1e-05) * ln_gain[...]).astype(BF16)
        for g in range(3):
            nbuf[g, pl.ds(start, size), :] = normed[:, g * 512:(g + 1) * 512]

    own_frames.wait()

    def norm_step(i, carry):
        norm(pl.multiple_of(EDGE + i * 32, 16), 32)
        return carry

    lax.fori_loop(0, ROWS // 32, norm_step, 0)
    arrived(xbuf.at[pl.ds(0, EDGE)], hs, 0)
    norm(0, EDGE)
    arrived(xbuf.at[pl.ds(EDGE + ROWS, EDGE)], hs, 1)
    norm(EDGE + ROWS, EDGE)

    own_rows[0].wait()
    own_rows[1].wait()
    x_wait(0, 0)
    y_send(0, 0)
    z_wait(0)
    x_send(0, 1)
    x_send(0, 2)
    x_wait(1, 0)
    y_send(1, 0)
    c_send(0, 0, 0)
    c_send(1, 0, 0)
    z_wait(1)
    x_send(1, 1)
    x_send(1, 2)
    for which in (1, 2):
        x_wait(0, which)
        y_send(0, which)
        c_send(0, which, 0)
    z_send(2)
    x_send(2, 0)
    for layer in (0, 1):
        y_wait(layer, 0)
        c_send(layer, 0, 1)
    for which in (1, 2):
        x_wait(1, which)
        y_send(1, which)
        c_send(1, which, 0)
    for layer in (0, 1):
        c_wait(layer, 0)

    def dot(g, m, size, cols):
        w = wbuf[g, :, :, :, cols].reshape(512, 256)
        return jnp.dot(nbuf[g, pl.ds(m, size), :], w, preferred_element_type=F32)

    def first_dot(j, carry):
        cols = pl.ds(pl.multiple_of(j * 256, 256), 256)
        acc[j] = dot(zh, 0, ALL, cols)
        return carry

    lax.fori_loop(0, 6, first_dot, 0)
    for layer in (0, 1):
        for which in (1, 2):
            y_wait(layer, which)
            c_send(layer, which, 1)
    z_wait(2)
    x_send(2, 1)
    x_send(2, 2)
    own_rows[2].wait()
    x_wait(2, 0)
    y_send(2, 0)
    c_send(2, 0, 0)
    for layer in (0, 1):
        for which in (1, 2):
            c_wait(layer, which)

    length = lengths[0]
    HM = ALL // 2

    def gate_step(i, carry):
        j, m = i // 2, i % 2
        m0 = pl.multiple_of(m * HM, 16)
        position = t * ROWS - EDGE + m0 + lax.broadcasted_iota(jnp.int32, (HM, 256), 0)
        valid = (position >= 0) & (position < length)
        pair = []
        for k in (0, 3):
            cols = pl.ds(pl.multiple_of((j + k) * 256, 256), 256)
            pair.append(acc[j + k, pl.ds(m0, HM), :] + (dot(up, m0, HM, cols) + dot(down, m0, HM, cols)))
        gated = jnp.where(valid, pair[0] * sigmoid(pair[1]), 0.0).astype(BF16).astype(F32)
        gbuf[j * 2, pl.ds(m0, HM), :] = gated[:, :128]
        gbuf[j * 2 + 1, pl.ds(m0, HM), :] = gated[:, 128:]
        return carry

    lax.fori_loop(0, 6, gate_step, 0)

    for which in (1, 2):
        x_wait(2, which)
        y_send(2, which)
        c_send(2, which, 0)

    local = jnp.clip(length - t * ROWS, 0, ROWS).astype(F32)
    BLOCK = 64

    def conv_step(s, carry):
        lanes = pl.ds(pl.multiple_of(s * 128, 128), 128)
        total = jnp.zeros((8, 128), F32)
        for b in range(0, ROWS, BLOCK):
            value = jnp.zeros((BLOCK, 128), F32)
            for k in range(TAPS):
                value = value + gbuf[s, pl.ds(b + 1 + k, BLOCK), :] * dw[pl.ds(k, 1), lanes]
            cbuf[s, pl.ds(b, BLOCK), :] = value
            position = t * ROWS + b + lax.broadcasted_iota(jnp.int32, (BLOCK, 128), 0)
            masked = jnp.where(position < length, value, 0.0)
            total = total + masked.reshape(BLOCK // 8, 8, 128).sum(axis=0)
        mean = total.sum(axis=0, keepdims=True) / jnp.maximum(local, 1.0)
        square = jnp.zeros((8, 128), F32)
        for b in range(0, ROWS, BLOCK):
            position = t * ROWS + b + lax.broadcasted_iota(jnp.int32, (BLOCK, 128), 0)
            delta = jnp.where(position < length, cbuf[s, pl.ds(b, BLOCK), :] - mean, 0.0)
            square = square + (delta * delta).reshape(BLOCK // 8, 8, 128).sum(axis=0)
        r1[slot1, pl.ds(s, 1), :] = mean
        r1[slot1, pl.ds(s + 8, 1), :] = square.sum(axis=0, keepdims=True)
        return carry

    r1[slot1] = jnp.zeros((16, 128), F32)
    lax.fori_loop(0, STRIPS, conv_step, 0)
    r1[slot1, pl.ds(6, 1), :] = jnp.full((1, 128), local, F32)

    def exchange(ref, slot, count, base, to):
        sems = (ssend, srecv)
        for d in range(1, count):
            send(ref.at[slot], ref.at[slot], sems, base + d, to(d))
        for d in range(1, count):
            arrived(ref.at[(slot + count - d) % count], sems, base + d)
        return combine(ref, count)

    mean, square = exchange(r1, slot1, 8, 0, peer1)
    r2[y, 0:8, :] = mean
    r2[y, 8:16, :] = square
    for which in (0, 1, 2):
        y_wait(2, which)
        c_send(2, which, 1)
    mean, square = exchange(r2, y, NY, 8, lambda d: at(dy=d))
    r3[z, 0:8, :] = mean
    r3[z, 8:16, :] = square
    mean, square = exchange(r3, z, NZ, 16, lambda d: at(dz=d))
    count = mean[6:7, :]
    scale = lax.rsqrt(square / count + 1e-05)
    for which in (0, 1, 2):
        c_wait(2, which)

    TM = 128
    final[0:8, :] = mean
    final[8:16, :] = scale

    def last_step(i, carry):
        m0 = pl.multiple_of(i * TM, TM)
        for s in range(STRIPS):
            lanes = slice(s * 128, (s + 1) * 128)
            factor = final[8 + s:9 + s, :] * bn_gain[:, lanes]
            value = (cbuf[s, pl.ds(m0, TM), :] - final[s:s + 1, :]) * factor + bn_shift[:, lanes]
            act[:, lanes] = (value * sigmoid(value)).astype(BF16)
        position = t * ROWS + m0 + lax.broadcasted_iota(jnp.int32, (TM, 512), 0)
        valid = position < length
        for j in range(3):
            w = vbuf[:, :, :, :, j * 512:(j + 1) * 512].reshape(CH, 512)
            res = jnp.dot(act[...], w, preferred_element_type=F32)
            out[0, pl.ds(m0, TM), j * 512:(j + 1) * 512] = jnp.where(valid, res, 0.0).astype(BF16)
        return carry

    lax.fori_loop(0, ROWS // TM, last_step, 0)
    for copy in sent:
        copy.wait_send()


def body(frames, lengths, ln_gain, w_in, dw_kernel, bn_gain, bn_shift, w_out):
    hbm = pl.BlockSpec(memory_space=pltpu.HBM)
    vmem = pl.BlockSpec(memory_space=pltpu.VMEM)
    smem = pl.BlockSpec(memory_space=pltpu.SMEM)
    return pl.pallas_call(
        kernel,
        out_shape=jax.ShapeDtypeStruct((1, ROWS, D), BF16),
        in_specs=[hbm, smem, vmem, hbm, vmem, vmem, vmem, hbm],
        out_specs=vmem,
        scratch_shapes=[
            pltpu.VMEM((ALL, D), BF16),
            pltpu.VMEM((3, ALL, 512), BF16),
            pltpu.VMEM((3, NX, 2, 64, D), BF16),
            pltpu.VMEM((3, NX, 2, 32, D), BF16),
            pltpu.VMEM((6, ALL, 256), F32),
            pltpu.VMEM((STRIPS, ALL, 128), F32),
            pltpu.VMEM((STRIPS, ROWS, 128), F32),
            pltpu.VMEM((128, CH), BF16),
            pltpu.VMEM((8, 16, 128), F32),
            pltpu.VMEM((NY, 16, 128), F32),
            pltpu.VMEM((NZ, 16, 128), F32),
            pltpu.VMEM((16, 128), F32),
            pltpu.SemaphoreType.DMA((LAYERS, SEMS)),
            pltpu.SemaphoreType.DMA((LAYERS, SEMS)),
            pltpu.SemaphoreType.DMA((2,)),
            pltpu.SemaphoreType.DMA((2,)),
            pltpu.SemaphoreType.DMA((28,)),
            pltpu.SemaphoreType.DMA((28,)),
            pltpu.SemaphoreType.DMA((4,)),
        ],
        compiler_params=pltpu.CompilerParams(
            collective_id=0, has_side_effects=True, vmem_limit_bytes=50 << 20
        ),
        name="conformer_conv",
    )(frames, lengths, ln_gain.reshape(1, D), w_in, dw_kernel, bn_gain.reshape(1, CH), bn_shift.reshape(1, CH), w_out)


def solution(mesh):
    return jax.shard_map(
        body,
        mesh=mesh,
        in_specs=(
            P("fsdp", "ctx", None),
            P("fsdp"),
            P(),
            P("fsdp", None),
            P(),
            P(),
            P(),
            P("fsdp", None),
        ),
        out_specs=P("fsdp", "ctx", None),
        check_vma=False,
    )
```

time: 372 us -> 83.4 us (0.22)
  blocking collectives: 227 us -> 0 us
  waiting for transfers between devices: 105 us -> 0 us
  Pallas kernels: 0 us -> 74.6 us
  between operations: 14.2 us -> 0.67 us
  other arithmetic: 11.7 us -> 0 us
  matrix products: 9.03 us -> 0 us
  local copies, waits for them, and re-layouts: 0.3 us -> 7.34 us
  starting transfers between devices: 4.44 us -> 0 us
    psum x2 -> x0, blocking collectives: 227 us -> none  [the longest x1 123 us: body(): lax.psum((jnp.sum(masked_conv, axis=(0, 1)), local_count), ('fsdp', 'ctx'))]
    all_gather x2 -> x0, waiting for transfers between devices: 101 us -> none  [the longest x1 101 us: body(): lax.all_gather(w_in, 'fsdp', axis=0, tiled=True)]
    pallas_call x0 -> x1, Pallas kernels: none -> 74.6 us  [body(): pl.pallas_call(kernel, out_shape=jax.ShapeDtypeStruct((1, ROWS, D), BF16)...]
    reduce_sum x5 -> x0, other arithmetic: 9.81 us -> none  [the longest x1 6.63 us: body(): jnp.sum(masked_conv, axis=(0, 1))]
    dot_general x2 -> x0, matrix products: 9.03 us -> none  [the longest x1 4.66 us: body(): jnp.dot(columns, lax.all_gather(w_in, 'fsdp', axis=0, tiled=True), prefer...]
    unnamed x10 -> x9, local copies, waits for them, and re-layouts: 0.02 us -> 5.26 us
    ppermute x2 -> x0, starting transfers between devices: 4.4 us -> none  [the longest x1 3.11 us: extended(): lax.ppermute(tail, axis, [(i, (i + 1) % count) for i in range(ends)])]
  transfers between devices with their start and end apart: 4 -> 0, of which waited for: 2 -> 0; matrix products, arithmetic and copies ran while one was open for 4% -> 0% of each run, Pallas kernels for 0% -> 0%
where the time goes in v1:
time: 83.4 us; the launch traced here: 82.6 us
  Pallas kernels  74.6 us (89%)
  local copies, waits for them, and re-layouts  7.34 us (9%)
    pallas_call x1, Pallas kernels, body(): pl.pallas_call(kernel, out_shape=jax.ShapeDtypeStruct((1, ROWS, D), BF16)...  74.6 us
    unnamed x9, local copies, waits for them, and re-layouts  5.26 us

profile of v1, /device:TPU:1, one launch (start us, length us, event | category | flops | bytes accessed | tf_op | source)
XLA Modules:
  0.0 82.6 jit_solution(7556556848267377513)
XLA Ops:
  0.7 0.7 reshape.10.bn_gain
  1.3 0.7 reshape.11.bn_shift
  2.0 0.7 reshape.9.ln_gain
  2.7 0.0 copy-start
  2.7 1.4 %copy-done = bf16[1,512,1536]{2,1,0:T(8,128)(2,1)S(1)} copy-done((bf16[1,512,1536]{2,1,0:T(8,128)(2,1)S(1)}, bf16[1,512,1536]{2,1,0:T(8,128)(2,1)}, u32[]{:S(2)}) %copy-start) | copy-done | bytes 1572888
  4.1 0.0 copy-start.1
  4.1 0.9 %copy-done.1 = bf16[64,1536]{1,0:T(8,128)(2,1)S(1)} copy-done((bf16[64,1536]{1,0:T(8,128)(2,1)S(1)}, bf16[64,1536]{1,0:T(8,128)(2,1)}, u32[]{:S(2)}) %copy-start.1) | copy-done | bytes 196632
  5.1 0.0 copy-start.2
  5.1 0.9 %copy-done.2 = f32[31,768]{1,0:T(8,128)S(1)} copy-done((f32[31,768]{1,0:T(8,128)S(1)}, f32[31,768]{1,0:T(8,128)}, u32[]{:S(2)}) %copy-start.2) | copy-done | bytes 95256
  6.0 0.0 copy-start.3
  6.0 0.9 %copy-done.3 = bf16[32,1536]{1,0:T(8,128)(2,1)S(1)} copy-done((bf16[32,1536]{1,0:T(8,128)(2,1)S(1)}, bf16[32,1536]{1,0:T(8,128)(2,1)}, u32[]{:S(2)}) %copy-start.3) | copy-done | bytes 98328
  6.9 74.6 %conformer_conv.1 = bf16[1,512,1536]{2,1,0:T(8,128)(2,1)S(1)} custom-call(bf16[1,512,1536]{2,1,0:T(8,128)(2,1)S(1)} %copy-done, s32[1]{0:T(128)S(6)} %copy.10.lengths, f32[1,1536]{1,0:T(1,128)S(1)} %reshape.9.ln_gain, bf16[64,1536]{1,0:T(8,128)(2,1)S(1)} %copy-done.1, f32[31,768]{1,0:T(8,128)S(1)} %copy-done.2, f32[1,768]{1,0:T(1,128)S(1)} %reshape.10.bn_gain, ...), custom_call_target="tpu_custom_call" | custom-call | tf_op jit(solution)/shard_map/conformer_conv/pallas_call | solution.py:355
  81.4 1.1 %copy.11 = bf16[1,512,1536]{2,1,0:T(8,128)(2,1)} copy(bf16[1,512,1536]{2,1,0:T(8,128)(2,1)S(1)} %conformer_conv.1) | data formatting | bytes 3145728
Async XLA Ops:
  2.7 1.4 %copy-start = (bf16[1,512,1536]{2,1,0:T(8,128)(2,1)S(1)}, bf16[1,512,1536]{2,1,0:T(8,128)(2,1)}, u32[]{:S(2)}) copy-start(bf16[1,512,1536]{2,1,0:T(8,128)(2,1)} %frames.1) | copy-start | bytes 4718596
  4.1 0.9 %copy-start.1 = (bf16[64,1536]{1,0:T(8,128)(2,1)S(1)}, bf16[64,1536]{1,0:T(8,128)(2,1)}, u32[]{:S(2)}) copy-start(bf16[64,1536]{1,0:T(8,128)(2,1)} %w_in.1) | copy-start | bytes 589828
  5.1 0.9 %copy-start.2 = (f32[31,768]{1,0:T(8,128)S(1)}, f32[31,768]{1,0:T(8,128)}, u32[]{:S(2)}) copy-start(f32[31,768]{1,0:T(8,128)} %dw.1) | copy-start | bytes 285700
  6.0 0.9 %copy-start.3 = (bf16[32,1536]{1,0:T(8,128)(2,1)S(1)}, bf16[32,1536]{1,0:T(8,128)(2,1)}, u32[]{:S(2)}) copy-start(bf16[32,1536]{1,0:T(8,128)(2,1)} %w_out.1) | copy-start | bytes 294916

commit v2 on v1

--- a/solution.py
+++ b/solution.py
@@ -14,8 +14,8 @@
 TAPS, CH, D = 31, 768, 1536
 STRIPS = CH // 128
 LAYERS = 3
-ZS, XS, YS, CS = 0, 2, 11, 17
-SEMS = 23
+ZS, XS, YS = 0, 2, 8
+XO, CS = 0, 3
 
 
 def device_of(x, y, z, c):
@@ -45,7 +45,7 @@
 def kernel(
     frames, lengths, ln_gain, w_in, dw, bn_gain, bn_shift, w_out, out,
     xbuf, nbuf, wbuf, vbuf, acc, gbuf, cbuf, act, r1, r2, r3, final,
-    gsend, grecv, hsend, hrecv, ssend, srecv, lsem,
+    gsend, grecv, qsend, qrecv, hsend, hrecv, ssend, srecv, lsem,
 ):
     f, t = lax.axis_index("fsdp"), lax.axis_index("ctx")
     x, c = (f // 2) % NX, f % 2
@@ -112,63 +112,80 @@
     def arrived(dst, sems, k):
         remote(dst, dst, sems, k, at(dc=1)).wait_recv()
 
-    def gs(layer):
-        return (gsend.at[layer], grecv.at[layer])
+    def gs(chunk):
+        return (gsend.at[chunk], grecv.at[chunk])
+
+    def qs(layer):
+        return (qsend.at[layer], qrecv.at[layer])
 
     XD = (1, 3, 2)
 
-    def unit(layer, group, xs):
-        return bufs[layer].at[group, xs, c, span(rows_of[layer])]
-
-    def z_send(layer):
+    def half(chunk):
+        return pl.ds((chunk % 2) * CH, CH)
+
+    def unit(chunk, group, xs):
+        layer = chunk // 2
+        return bufs[layer].at[group, xs, c, span(rows_of[layer]), half(chunk)]
+
+    def z_send(chunk):
+        src = shards[chunk // 2].at[span(rows_of[chunk // 2]), half(chunk)]
+        dst = unit(chunk, zh, x)
+        send(src, dst, gs(chunk), ZS + 0, at(dz=-4))
+        send(src, dst, gs(chunk), ZS + 1, at(dz=4))
+
+    def z_wait(chunk):
+        arrived(unit(chunk, up, x), gs(chunk), ZS + 0)
+        arrived(unit(chunk, down, x), gs(chunk), ZS + 1)
+
+    def xo_send(layer):
         src = shards[layer].at[span(rows_of[layer])]
-        dst = unit(layer, zh, x)
-        send(src, dst, gs(layer), ZS + 0, at(dz=-4))
-        send(src, dst, gs(layer), ZS + 1, at(dz=4))
-
-    def z_wait(layer):
-        arrived(unit(layer, up, x), gs(layer), ZS + 0)
-        arrived(unit(layer, down, x), gs(layer), ZS + 1)
-
-    def x_send(layer, which):
-        dst = unit(layer, groups[which], x)
-        src = shards[layer].at[span(rows_of[layer])] if which == 0 else dst
+        dst = bufs[layer].at[zh, x, c, span(rows_of[layer])]
         for i, d in enumerate(XD):
-            send(src, dst, gs(layer), XS + which * 3 + i, at(dx=d))
-
-    def x_wait(layer, which):
+            send(src, dst, qs(layer), XO + i, at(dx=d))
+
+    def xo_wait(layer):
         for i, d in enumerate(XD):
-            arrived(unit(layer, groups[which], (x + 4 - d) % NX), gs(layer), XS + which * 3 + i)
-
-    def piece(layer, group, rows, side):
-        return bufs[layer].at[group, :, c, span(rows), pl.ds(side * CH, CH)]
-
-    def y_send(layer, which):
-        for side, d in ((0, 1), (1, 7)):
-            ref = piece(layer, groups[which], rows_of[layer], side)
-            send(ref, ref, gs(layer), YS + which * 2 + side, at(dy=d))
-
-    def y_wait(layer, which):
-        for side in (0, 1):
-            arrived(piece(layer, groups[which], other_of[layer], side), gs(layer), YS + which * 2 + side)
-
-    def block(layer, group, core, rows):
-        return bufs[layer].at[group, :, core, span(rows)]
-
-    def c_send(layer, which, half):
-        rows = (rows_of, other_of)[half][layer]
-        ref = block(layer, groups[which], c, rows)
-        send(ref, ref, gs(layer), CS + which * 2 + half, at(dc=1))
+            dst = bufs[layer].at[zh, (x + 4 - d) % NX, c, span(rows_of[layer])]
+            arrived(dst, qs(layer), XO + i)
+
+    def xf_send(chunk):
+        for which in (1, 2):
+            ref = unit(chunk, groups[which], x)
+            for i, d in enumerate(XD):
+                send(ref, ref, gs(chunk), XS + (which - 1) * 3 + i, at(dx=d))
+
+    def xf_wait(chunk):
+        for which in (1, 2):
+            for i, d in enumerate(XD):
+                ref = unit(chunk, groups[which], (x + 4 - d) % NX)
+                arrived(ref, gs(chunk), XS + (which - 1) * 3 + i)
+
+    def piece(chunk, which, rows):
+        layer = chunk // 2
+        return bufs[layer].at[groups[which], :, c, span(rows[layer]), half(chunk)]
+
+    def y_send(chunk, which):
+        ref = piece(chunk, which, rows_of)
+        send(ref, ref, gs(chunk), YS + which, at(dy=(1, 7)[chunk % 2]))
+
+    def y_wait(chunk, which):
+        arrived(piece(chunk, which, other_of), gs(chunk), YS + which)
+
+    def c_send(layer, which, part):
+        rows = (rows_of, other_of)[part][layer]
+        ref = bufs[layer].at[groups[which], :, c, span(rows)]
+        send(ref, ref, qs(layer), CS + which * 2 + part, at(dc=1))
 
     def c_wait(layer, which):
-        for half in (0, 1):
-            rows = (rows_of, other_of)[half][layer]
-            arrived(block(layer, groups[which], 1 - c, rows), gs(layer), CS + which * 2 + half)
+        for part in (0, 1):
+            rows = (rows_of, other_of)[part][layer]
+            ref = bufs[layer].at[groups[which], :, 1 - c, span(rows)]
+            arrived(ref, qs(layer), CS + which * 2 + part)
 
     z_send(0)
-    x_send(0, 0)
     z_send(1)
-    x_send(1, 0)
+    xo_send(0)
+    xo_send(1)
     hs = (hsend, hrecv)
     send(frames.at[0, pl.ds(ROWS - EDGE, EDGE)], xbuf.at[pl.ds(0, EDGE)], hs, 0, right)
     send(frames.at[0, pl.ds(0, EDGE)], xbuf.at[pl.ds(EDGE + ROWS, EDGE)], hs, 1, left)
@@ -178,7 +195,7 @@
         centre = jnp.mean(values, axis=-1, keepdims=True)
         deviate = values - centre
         spread = jnp.mean(deviate * deviate, axis=-1, keepdims=True)
-        normed = (deviate * lax.rsqrt(spread + 1e-05) * ln_gain[...]).astype(BF16)
+        normed = (deviate * lax.rsqrt(spread + 1e-05) * ln_gain[...].reshape(1, D)).astype(BF16)
         for g in range(3):
             nbuf[g, pl.ds(start, size), :] = normed[:, g * 512:(g + 1) * 512]
 
@@ -194,36 +211,6 @@
     arrived(xbuf.at[pl.ds(EDGE + ROWS, EDGE)], hs, 1)
     norm(EDGE + ROWS, EDGE)
 
-    own_rows[0].wait()
-    own_rows[1].wait()
-    x_wait(0, 0)
-    y_send(0, 0)
-    z_wait(0)
-    x_send(0, 1)
-    x_send(0, 2)
-    x_wait(1, 0)
-    y_send(1, 0)
-    c_send(0, 0, 0)
-    c_send(1, 0, 0)
-    z_wait(1)
-    x_send(1, 1)
-    x_send(1, 2)
-    for which in (1, 2):
-        x_wait(0, which)
-        y_send(0, which)
-        c_send(0, which, 0)
-    z_send(2)
-    x_send(2, 0)
-    for layer in (0, 1):
-        y_wait(layer, 0)
-        c_send(layer, 0, 1)
-    for which in (1, 2):
-        x_wait(1, which)
-        y_send(1, which)
-        c_send(1, which, 0)
-    for layer in (0, 1):
-        c_wait(layer, 0)
-
     def dot(g, m, size, cols):
         w = wbuf[g, :, :, :, cols].reshape(512, 256)
         return jnp.dot(nbuf[g, pl.ds(m, size), :], w, preferred_element_type=F32)
@@ -233,17 +220,62 @@
         acc[j] = dot(zh, 0, ALL, cols)
         return carry
 
+    z_wait(0)
+    z_send(2)
+    xf_send(0)
+    own_rows[0].wait()
+    own_rows[1].wait()
+    xo_wait(0)
+    xo_wait(1)
+    for chunk in range(4):
+        y_send(chunk, 0)
+    z_wait(1)
+    z_send(3)
+    xf_send(1)
+    c_send(0, 0, 0)
+    c_send(1, 0, 0)
+    z_wait(2)
+    xf_send(2)
+    xf_wait(0)
+    y_send(0, 1)
+    y_send(0, 2)
+    z_wait(3)
+    xf_send(3)
+    z_send(4)
+    z_send(5)
+    xf_wait(1)
+    y_send(1, 1)
+    y_send(1, 2)
+    c_send(0, 1, 0)
+    c_send(0, 2, 0)
+    for chunk in range(4):
+        y_wait(chunk, 0)
+    c_send(0, 0, 1)
+    c_send(1, 0, 1)
+    xf_wait(2)
+    y_send(2, 1)
+    y_send(2, 2)
+    xo_send(2)
+    for layer in (0, 1):
+        c_wait(layer, 0)
     lax.fori_loop(0, 6, first_dot, 0)
+    xf_wait(3)
+    for which in (1, 2):
+        y_send(3, which)
+        c_send(1, which, 0)
     for layer in (0, 1):
         for which in (1, 2):
-            y_wait(layer, which)
+            y_wait(2 * layer, which)
+            y_wait(2 * layer + 1, which)
             c_send(layer, which, 1)
-    z_wait(2)
-    x_send(2, 1)
-    x_send(2, 2)
+    z_wait(4)
+    z_wait(5)
+    xf_send(4)
+    xf_send(5)
     own_rows[2].wait()
-    x_wait(2, 0)
-    y_send(2, 0)
+    xo_wait(2)
+    y_send(4, 0)
+    y_send(5, 0)
     c_send(2, 0, 0)
     for layer in (0, 1):
         for which in (1, 2):
@@ -268,9 +300,11 @@
 
     lax.fori_loop(0, 6, gate_step, 0)
 
+    xf_wait(4)
+    xf_wait(5)
     for which in (1, 2):
-        x_wait(2, which)
-        y_send(2, which)
+        y_send(4, which)
+        y_send(5, which)
         c_send(2, which, 0)
 
     local = jnp.clip(length - t * ROWS, 0, ROWS).astype(F32)
@@ -313,7 +347,8 @@
     r2[y, 0:8, :] = mean
     r2[y, 8:16, :] = square
     for which in (0, 1, 2):
-        y_wait(2, which)
+        y_wait(4, which)
+        y_wait(5, which)
         c_send(2, which, 1)
     mean, square = exchange(r2, y, NY, 8, lambda d: at(dy=d))
     r3[z, 0:8, :] = mean
@@ -332,8 +367,8 @@
         m0 = pl.multiple_of(i * TM, TM)
         for s in range(STRIPS):
             lanes = slice(s * 128, (s + 1) * 128)
-            factor = final[8 + s:9 + s, :] * bn_gain[:, lanes]
-            value = (cbuf[s, pl.ds(m0, TM), :] - final[s:s + 1, :]) * factor + bn_shift[:, lanes]
+            factor = final[8 + s:9 + s, :] * bn_gain[lanes].reshape(1, 128)
+            value = (cbuf[s, pl.ds(m0, TM), :] - final[s:s + 1, :]) * factor + bn_shift[lanes].reshape(1, 128)
             act[:, lanes] = (value * sigmoid(value)).astype(BF16)
         position = t * ROWS + m0 + lax.broadcasted_iota(jnp.int32, (TM, 512), 0)
         valid = position < length
@@ -370,8 +405,10 @@
             pltpu.VMEM((NY, 16, 128), F32),
             pltpu.VMEM((NZ, 16, 128), F32),
             pltpu.VMEM((16, 128), F32),
-            pltpu.SemaphoreType.DMA((LAYERS, SEMS)),
-            pltpu.SemaphoreType.DMA((LAYERS, SEMS)),
+            pltpu.SemaphoreType.DMA((2 * LAYERS, 11)),
+            pltpu.SemaphoreType.DMA((2 * LAYERS, 11)),
+            pltpu.SemaphoreType.DMA((LAYERS, 9)),
+            pltpu.SemaphoreType.DMA((LAYERS, 9)),
             pltpu.SemaphoreType.DMA((2,)),
             pltpu.SemaphoreType.DMA((2,)),
             pltpu.SemaphoreType.DMA((28,)),
@@ -379,10 +416,10 @@
             pltpu.SemaphoreType.DMA((4,)),
         ],
         compiler_params=pltpu.CompilerParams(
-            collective_id=0, has_side_effects=True, vmem_limit_bytes=50 << 20
+            collective_id=0, has_side_effects=True, vmem_limit_bytes=63 << 20
         ),
         name="conformer_conv",
-    )(frames, lengths, ln_gain.reshape(1, D), w_in, dw_kernel, bn_gain.reshape(1, CH), bn_shift.reshape(1, CH), w_out)
+    )(frames, lengths, ln_gain, w_in, dw_kernel, bn_gain, bn_shift, w_out)
 
 
 def solution(mesh):

time: 83.4 us -> 79.3 us (0.951)
  local copies, waits for them, and re-layouts: 7.34 us -> 2.65 us
  Pallas kernels: 74.6 us -> 75.6 us
    unnamed x9 -> x1, local copies, waits for them, and re-layouts: 5.26 us -> 2.65 us
    reshape x3 -> x0, local copies, waits for them, and re-layouts: 2.08 us -> none  [the longest x1 0.7 us: body(): ln_gain.reshape(1, D)]
    pallas_call x1, Pallas kernels: 74.6 us -> 75.6 us  [body(): pl.pallas_call(kernel, out_shape=jax.ShapeDtypeStruct((1, ROWS, D), BF16)...]
where the time goes in v2:
time: 79.3 us; the launch traced here: 78.9 us
  Pallas kernels  75.6 us (95%)
  local copies, waits for them, and re-layouts  2.65 us (3%)
    pallas_call x1, Pallas kernels, body(): pl.pallas_call(kernel, out_shape=jax.ShapeDtypeStruct((1, ROWS, D), BF16)...  75.6 us
    unnamed x1, local copies, waits for them, and re-layouts  2.65 us

profile of v2, /device:TPU:1, one launch (start us, length us, event | category | flops | bytes accessed | tf_op | source)
XLA Modules:
  0.0 78.9 jit_solution(10613874018041893958)
XLA Ops:
  0.7 75.6 %conformer_conv.1 = bf16[1,512,1536]{2,1,0:T(8,128)(2,1)} custom-call(bf16[1,512,1536]{2,1,0:T(8,128)(2,1)} %frames.1, s32[1]{0:T(128)S(6)} %copy.10.lengths, f32[1536]{0:T(1024)} %ln_gain.1, bf16[64,1536]{1,0:T(8,128)(2,1)} %w_in.1, f32[31,768]{1,0:T(8,128)} %dw.1, f32[768]{0:T(1024)} %bn_gain.1, f32[768]{0:T(1024)} %bn_shift.1, bf16[32,1536]{1,0:T(8,128)(2,1)} %w_out.1), custom_call_target="tpu_custom_call" | custom-call | tf_op jit(solution)/shard_map/conformer_conv/pallas_call | solution.py:390
  76.2 2.7 %copy.11 = bf16[1,512,1536]{2,1,0:T(8,128)(2,1)} copy(bf16[1,512,1536]{2,1,0:T(8,128)(2,1)} %conformer_conv.1) | data formatting | bytes 3145728

commit v3 on v1

v3 whole, which is shorter than its diff:
```python
import jax
import jax.numpy as jnp
from jax import lax
from jax.experimental import pallas as pl
from jax.experimental.pallas import tpu as pltpu
from jax.sharding import PartitionSpec as P

MESH = pl.DeviceIdType.MESH
BF16 = jnp.bfloat16
F32 = jnp.float32
NX, NY, NZ = 4, 8, 12
ROWS, EDGE = 512, 16
ALL = ROWS + 2 * EDGE
TAPS, CH, D = 31, 768, 1536
STRIPS = CH // 128


def device_of(x, y, z, c):
    return (((z // 4) * NX + x) * 2 + c, (z % 4) * NY + y)


def sigmoid(v):
    return 0.5 * jnp.tanh(0.5 * v) + 0.5


def combine(all_ref, parts):
    means = [all_ref[i, 0:8, :] for i in range(parts)]
    counts = [all_ref[i, 6:7, :] for i in range(parts)]
    squares = [all_ref[i, 8:16, :] for i in range(parts)]
    total = sum(counts[1:], counts[0])
    inverse = 1.0 / jnp.maximum(total, 1.0)
    weighted = [m * n for m, n in zip(means, counts)]
    mean = sum(weighted[1:], weighted[0]) * inverse
    spread = sum(squares[1:], squares[0])
    for m, n in zip(means, counts):
        spread = spread + n * (m - mean) * (m - mean)
    row = lax.broadcasted_iota(jnp.int32, (8, 128), 0)
    mean = jnp.where(row == 6, jnp.broadcast_to(total, (8, 128)), mean)
    return mean, spread


def kernel(
    frames, lengths, ln_gain, w_in, dw, bn_gain, bn_shift, w_out, out,
    xbuf, nbuf, wbuf, vbuf, acc, gbuf, cbuf, act, r1, r2, r3, final,
    gsend, grecv, qsend, qrecv, vsend, vrecv, hsend, hrecv, ssend, srecv, lsem,
):
    f, t = lax.axis_index("fsdp"), lax.axis_index("ctx")
    x, c = (f // 2) % NX, f % 2
    y = t % NY
    zh, zl = f // (2 * NX), t // NY
    z = zh * 4 + zl
    par = y % 2
    up, down = (zh + 1) % 3, (zh + 2) % 3
    groups = (zh, up, down)

    def at(dx=0, dy=0, dz=0, dc=0):
        return device_of((x + dx) % NX, (y + dy) % NY, (z + dz) % NZ, (c + dc) % 2)

    left, right = (f, (t + 31) % 32), (f, (t + 1) % 32)
    slot1 = x * 2 + c

    def peer1(d):
        to = (slot1 + d) % 8
        return device_of(to // 2, y, z, to % 2)

    peers = [left, right]
    peers += [peer1(d) for d in range(1, 8)]
    peers += [at(dy=d) for d in range(1, NY)]
    peers += [at(dz=d) for d in range(1, NZ)]

    mine_in = pl.ds(pl.multiple_of(par * 32, 32), 32)
    other_in = pl.ds(pl.multiple_of((1 - par) * 32, 32), 32)
    mine_out = pl.ds(pl.multiple_of(par * 16, 16), 16)
    other_out = pl.ds(pl.multiple_of((1 - par) * 16, 16), 16)
    direct, split = pl.ds(0, 3), pl.ds(3, 3)
    far = pl.ds(1, 2)

    own_frames = pltpu.make_async_copy(frames.at[0], xbuf.at[pl.ds(EDGE, ROWS)], lsem.at[0])
    own_frames.start()
    own_in, own_out = [], []
    for j in range(STRIPS):
        for side in (0, 1):
            cols = pl.ds(side * CH + j * 128, 128)
            src, dst = w_in.at[:, cols], wbuf.at[0, x, c, j, side]
            if j >= 3:
                src, dst = w_in.at[mine_in, cols], wbuf.at[0, x, c, j, side, mine_in]
            own_in.append(pltpu.make_async_copy(src, dst, lsem.at[1 + len(own_in)]))
    for side in (0, 1):
        src = w_out.at[mine_out, pl.ds(side * CH, CH)]
        own_out.append(pltpu.make_async_copy(src, vbuf.at[0, x, c, side, mine_out], lsem.at[13 + side]))
    for copy in own_in + own_out:
        copy.start()

    barrier = pltpu.get_barrier_semaphore()
    for peer in peers:
        pl.semaphore_signal(barrier, inc=1, device_id=peer, device_id_type=MESH)
    pl.semaphore_wait(barrier, len(peers))

    sent = []

    def remote(src, dst, sems, k, to):
        return pltpu.make_async_remote_copy(
            src_ref=src, dst_ref=dst, send_sem=sems[0].at[k], recv_sem=sems[1].at[k],
            device_id=to, device_id_type=MESH,
        )

    def send(*args):
        remote(*args).start()
        if args[2][0] is hsend or args[2][0] is ssend:
            sent.append(args)

    def arrived(dst, sems, k):
        remote(dst, dst, sems, k, at(dc=1)).wait_recv()

    XD = (1, 3, 2)

    def gs(j):
        return (gsend.at[j], grecv.at[j])

    qs = (qsend, qrecv)

    def z_send(j):
        src = wbuf.at[0, x, c, j, :, mine_in]
        send(src, wbuf.at[1, x, c, j, :, mine_in], gs(j), 0, at(dz=-4))
        send(src, wbuf.at[2, x, c, j, :, mine_in], gs(j), 1, at(dz=4))

    def z_wait(j):
        arrived(wbuf.at[1, x, c, j, :, mine_in], gs(j), 0)
        arrived(wbuf.at[2, x, c, j, :, mine_in], gs(j), 1)

    def x_send(j):
        ref = wbuf.at[far, x, c, j, :, mine_in]
        for i, d in enumerate(XD):
            send(ref, ref, gs(j), 2 + i, at(dx=d))

    def x_wait(j):
        for i, d in enumerate(XD):
            arrived(wbuf.at[far, (x + 4 - d) % NX, c, j, :, mine_in], gs(j), 2 + i)

    def y_send(j):
        for side, d in ((0, 1), (1, 7)):
            ref = wbuf.at[far, :, c, j, side, mine_in]
            send(ref, ref, gs(j), 5 + side, at(dy=d))

    def y_wait(j):
        for side in (0, 1):
            arrived(wbuf.at[far, :, c, j, side, other_in], gs(j), 5 + side)

    def c_send(j, part):
        ref = wbuf.at[far, :, c, j, :, (mine_in, other_in)[part]]
        send(ref, ref, gs(j), 7 + part, at(dc=1))

    def c_wait(j):
        for part in (0, 1):
            arrived(wbuf.at[far, :, 1 - c, j, :, (mine_in, other_in)[part]], gs(j), 7 + part)

    def xo_send():
        first, second = wbuf.at[0, x, c, direct], wbuf.at[0, x, c, split, :, mine_in]
        for i, d in enumerate(XD):
            send(first, first, qs, i, at(dx=d))
        for i, d in enumerate(XD):
            send(second, second, qs, 3 + i, at(dx=d))

    def xo_wait():
        for i, d in enumerate(XD):
            source = (x + 4 - d) % NX
            arrived(wbuf.at[0, source, c, direct], qs, i)
            arrived(wbuf.at[0, source, c, split, :, mine_in], qs, 3 + i)

    def own_y_send():
        for side, d in ((0, 1), (1, 7)):
            ref = wbuf.at[0, :, c, split, side, mine_in]
            send(ref, ref, qs, 6 + side, at(dy=d))

    def own_y_wait():
        for side in (0, 1):
            arrived(wbuf.at[0, :, c, split, side, other_in], qs, 6 + side)

    def own_part(part, core):
        if part == 0:
            return wbuf.at[0, :, core, direct]
        return wbuf.at[0, :, core, split, :, (mine_in, other_in)[part - 1]]

    def own_c_send(part):
        ref = own_part(part, c)
        send(ref, ref, qs, 8 + part, at(dc=1))

    def own_c_wait():
        for part in (0, 1, 2):
            arrived(own_part(part, 1 - c), qs, 8 + part)

    vs = (vsend, vrecv)

    def v_start():
        src = vbuf.at[0, x, c, :, mine_out]
        send(src, vbuf.at[1, x, c, :, mine_out], vs, 0, at(dz=-4))
        send(src, vbuf.at[2, x, c, :, mine_out], vs, 1, at(dz=4))
        for i, d in enumerate(XD):
            send(src, src, vs, 2 + i, at(dx=d))

    def v_x_send():
        arrived(vbuf.at[1, x, c, :, mine_out], vs, 0)
        arrived(vbuf.at[2, x, c, :, mine_out], vs, 1)
        ref = vbuf.at[far, x, c, :, mine_out]
        for i, d in enumerate(XD):
            send(ref, ref, vs, 5 + i, at(dx=d))

    def v_y_send():
        for i, d in enumerate(XD):
            source = (x + 4 - d) % NX
            arrived(vbuf.at[0, source, c, :, mine_out], vs, 2 + i)
            arrived(vbuf.at[far, source, c, :, mine_out], vs, 5 + i)
        for side, d in ((0, 1), (1, 7)):
            ref = vbuf.at[:, :, c, side, mine_out]
            send(ref, ref, vs, 8 + side, at(dy=d))
        ref = vbuf.at[:, :, c, :, mine_out]
        send(ref, ref, vs, 10, at(dc=1))

    def v_c_send():
        for side in (0, 1):
            arrived(vbuf.at[:, :, c, side, other_out], vs, 8 + side)
        ref = vbuf.at[:, :, c, :, other_out]
        send(ref, ref, vs, 11, at(dc=1))

    def v_wait():
        arrived(vbuf.at[:, :, 1 - c, :, mine_out], vs, 10)
        arrived(vbuf.at[:, :, 1 - c, :, other_out], vs, 11)

    for copy in own_in + own_out:
        copy.wait()
    z_send(0)
    z_send(1)
    xo_send()
    hs = (hsend, hrecv)
    send(frames.at[0, pl.ds(ROWS - EDGE, EDGE)], xbuf.at[pl.ds(0, EDGE)], hs, 0, right)
    send(frames.at[0, pl.ds(0, EDGE)], xbuf.at[pl.ds(EDGE + ROWS, EDGE)], hs, 1, left)

    def norm(start, size):
        values = xbuf[pl.ds(start, size), :].astype(F32)
        centre = jnp.mean(values, axis=-1, keepdims=True)
        deviate = values - centre
        spread = jnp.mean(deviate * deviate, axis=-1, keepdims=True)
        normed = (deviate * lax.rsqrt(spread + 1e-05) * ln_gain[...].reshape(1, D)).astype(BF16)
        for g in range(3):
            nbuf[g, pl.ds(start, size), :] = normed[:, g * 512:(g + 1) * 512]

    own_frames.wait()

    def norm_step(i, carry):
        norm(pl.multiple_of(EDGE + i * 32, 16), 32)
        return carry

    lax.fori_loop(0, ROWS // 32, norm_step, 0)
    arrived(xbuf.at[pl.ds(0, EDGE)], hs, 0)
    norm(0, EDGE)
    arrived(xbuf.at[pl.ds(EDGE + ROWS, EDGE)], hs, 1)
    norm(EDGE + ROWS, EDGE)

    def dot(g, j, m, size):
        w = [wbuf[g, :, :, j, side].reshape(512, 128) for side in (0, 1)]
        rows = nbuf[(zh + g) % 3, pl.ds(m, size), :]
        return jnp.dot(rows, jnp.concatenate(w, axis=1), preferred_element_type=F32)

    def first_dot(j, carry):
        acc[j] = dot(0, j, 0, ALL)
        return carry

    length = lengths[0]
    HM = ALL // 2

    def gate_step(j):
        def half(m, carry):
            m0 = pl.multiple_of(m * HM, 16)
            position = t * ROWS - EDGE + m0 + lax.broadcasted_iota(jnp.int32, (HM, 128), 0)
            valid = (position >= 0) & (position < length)
            pair = acc[j, pl.ds(m0, HM), :] + (dot(1, j, m0, HM) + dot(2, j, m0, HM))
            gated = jnp.where(valid, pair[:, :128] * sigmoid(pair[:, 128:]), 0.0)
            gbuf[j, pl.ds(m0, HM), :] = gated.astype(BF16).astype(F32)
            return carry

        lax.fori_loop(0, 2, half, 0)

    local = jnp.clip(length - t * ROWS, 0, ROWS).astype(F32)
    BLOCK = 64

    def conv_step(s):
        lanes = pl.ds(pl.multiple_of(s * 128, 128), 128)
        total = jnp.zeros((8, 128), F32)
        for b in range(0, ROWS, BLOCK):
            value = jnp.zeros((BLOCK, 128), F32)
            for k in range(TAPS):
                value = value + gbuf[s, pl.ds(b + 1 + k, BLOCK), :] * dw[pl.ds(k, 1), lanes]
            cbuf[s, pl.ds(b, BLOCK), :] = value
            position = t * ROWS + b + lax.broadcasted_iota(jnp.int32, (BLOCK, 128), 0)
            masked = jnp.where(position < length, value, 0.0)
            total = total + masked.reshape(BLOCK // 8, 8, 128).sum(axis=0)
        mean = total.sum(axis=0, keepdims=True) / jnp.maximum(local, 1.0)
        square = jnp.zeros((8, 128), F32)
        for b in range(0, ROWS, BLOCK):
            position = t * ROWS + b + lax.broadcasted_iota(jnp.int32, (BLOCK, 128), 0)
            delta = jnp.where(position < length, cbuf[s, pl.ds(b, BLOCK), :] - mean, 0.0)
            square = square + (delta * delta).reshape(BLOCK // 8, 8, 128).sum(axis=0)
        r1[slot1, pl.ds(s, 1), :] = mean
        r1[slot1, pl.ds(s + 8, 1), :] = square.sum(axis=0, keepdims=True)

    r1[slot1] = jnp.zeros((16, 128), F32)

    X_LAG, Y_LAG, C_LAG = 3, 6, 7

    def pipeline(i, carry):
        @pl.when(i < STRIPS)
        def _():
            z_wait(i)
            x_send(i)

        @pl.when(i < STRIPS - 2)
        def _():
            z_send(i + 2)

        @pl.when((i >= X_LAG) & (i < STRIPS + X_LAG))
        def _():
            x_wait(i - X_LAG)
            y_send(i - X_LAG)
            c_send(i - X_LAG, 0)

        @pl.when(i == 2)
        def _():
            xo_wait()
            own_y_send()
            own_c_send(0)
            own_c_send(1)

        @pl.when(i == 6)
        def _():
            v_start()
            own_y_wait()
            own_c_send(2)

        @pl.when((i >= Y_LAG) & (i < STRIPS + Y_LAG))
        def _():
            y_wait(i - Y_LAG)
            c_send(i - Y_LAG, 1)

        @pl.when(i == 7)
        def _():
            own_c_wait()
            lax.fori_loop(0, STRIPS, first_dot, 0)

        @pl.when(i == 9)
        def _():
            v_x_send()

        @pl.when(i == 12)
        def _():
            v_y_send()

        @pl.when(i >= C_LAG)
        def _():
            j = i - C_LAG
            c_wait(j)
            gate_step(j)
            conv_step(j)

        return carry

    lax.fori_loop(0, STRIPS + C_LAG, pipeline, 0)
    r1[slot1, pl.ds(6, 1), :] = jnp.full((1, 128), local, F32)

    def exchange(ref, slot, count, base, to, between=None):
        sems = (ssend, srecv)
        for d in range(1, count):
            send(ref.at[slot], ref.at[slot], sems, base + d, to(d))
        if between is not None:
            between()
        for d in range(1, count):
            arrived(ref.at[(slot + count - d) % count], sems, base + d)
        return combine(ref, count)

    mean, square = exchange(r1, slot1, 8, 0, peer1)
    r2[y, 0:8, :] = mean
    r2[y, 8:16, :] = square
    mean, square = exchange(r2, y, NY, 8, lambda d: at(dy=d))
    r3[z, 0:8, :] = mean
    r3[z, 8:16, :] = square
    mean, square = exchange(r3, z, NZ, 16, lambda d: at(dz=d), v_c_send)
    count = mean[6:7, :]
    scale = lax.rsqrt(square / count + 1e-05)
    v_wait()

    TM = 128
    final[0:8, :] = mean
    final[8:16, :] = scale

    def last_step(i, carry):
        m0 = pl.multiple_of(i * TM, TM)
        for s in range(STRIPS):
            lanes = slice(s * 128, (s + 1) * 128)
            factor = final[8 + s:9 + s, :] * bn_gain[lanes].reshape(1, 128)
            value = (cbuf[s, pl.ds(m0, TM), :] - final[s:s + 1, :]) * factor + bn_shift[lanes].reshape(1, 128)
            act[s // 2, :, (s % 2) * 128:(s % 2 + 1) * 128] = (value * sigmoid(value)).astype(BF16)
        position = t * ROWS + m0 + lax.broadcasted_iota(jnp.int32, (TM, CH), 0)
        valid = position < length
        for side in (0, 1):
            res = 0.0
            for g in range(3):
                w = vbuf[g, :, :, side].reshape(256, CH)
                res = res + jnp.dot(act[(zh + g) % 3], w, preferred_element_type=F32)
            out[0, pl.ds(m0, TM), side * CH:(side + 1) * CH] = jnp.where(valid, res, 0.0).astype(BF16)
        return carry

    lax.fori_loop(0, ROWS // TM, last_step, 0)
    def drain(j, carry):
        src = wbuf.at[0, x, c, j, :, mine_in]
        for k in (0, 1):
            remote(src, src, gs(j), k, at(dc=1)).wait_send()
        for k in (2, 3, 4):
            ref = wbuf.at[far, x, c, j, :, mine_in]
            remote(ref, ref, gs(j), k, at(dc=1)).wait_send()
        for side in (0, 1):
            ref = wbuf.at[far, :, c, j, side, mine_in]
            remote(ref, ref, gs(j), 5 + side, at(dc=1)).wait_send()
        for part in (0, 1):
            ref = wbuf.at[far, :, c, j, :, (mine_in, other_in)[part]]
            remote(ref, ref, gs(j), 7 + part, at(dc=1)).wait_send()
        return carry

    lax.fori_loop(0, STRIPS, drain, 0)
    leaving = [(wbuf.at[0, x, c, direct], qs, k) for k in (0, 1, 2)]
    leaving += [(wbuf.at[0, x, c, split, :, mine_in], qs, k) for k in (3, 4, 5)]
    leaving += [(wbuf.at[0, :, c, split, side, mine_in], qs, 6 + side) for side in (0, 1)]
    leaving += [(own_part(part, c), qs, 8 + part) for part in (0, 1, 2)]
    leaving += [(vbuf.at[0, x, c, :, mine_out], vs, k) for k in range(5)]
    leaving += [(vbuf.at[far, x, c, :, mine_out], vs, k) for k in (5, 6, 7)]
    leaving += [(vbuf.at[:, :, c, side, mine_out], vs, 8 + side) for side in (0, 1)]
    leaving += [(vbuf.at[:, :, c, :, rows], vs, 10 + k) for k, rows in enumerate((mine_out, other_out))]
    for ref, sems, k in leaving:
        remote(ref, ref, sems, k, at(dc=1)).wait_send()
    for args in sent:
        remote(*args).wait_send()


def body(frames, lengths, ln_gain, w_in, dw_kernel, bn_gain, bn_shift, w_out):
    hbm = pl.BlockSpec(memory_space=pltpu.HBM)
    vmem = pl.BlockSpec(memory_space=pltpu.VMEM)
    smem = pl.BlockSpec(memory_space=pltpu.SMEM)
    return pl.pallas_call(
        kernel,
        out_shape=jax.ShapeDtypeStruct((1, ROWS, D), BF16),
        in_specs=[hbm, smem, vmem, hbm, vmem, vmem, vmem, hbm],
        out_specs=vmem,
        scratch_shapes=[
            pltpu.VMEM((ALL, D), BF16),
            pltpu.VMEM((3, ALL, 512), BF16),
            pltpu.VMEM((3, NX, 2, STRIPS, 2, 64, 128), BF16),
            pltpu.VMEM((3, NX, 2, 2, 32, CH), BF16),
            pltpu.VMEM((6, ALL, 256), F32),
            pltpu.VMEM((STRIPS, ALL, 128), F32),
            pltpu.VMEM((STRIPS, ROWS, 128), F32),
            pltpu.VMEM((3, 128, 256), BF16),
            pltpu.VMEM((8, 16, 128), F32),
            pltpu.VMEM((NY, 16, 128), F32),
            pltpu.VMEM((NZ, 16, 128), F32),
            pltpu.VMEM((16, 128), F32),
            pltpu.SemaphoreType.DMA((STRIPS, 9)),
            pltpu.SemaphoreType.DMA((STRIPS, 9)),
            pltpu.SemaphoreType.DMA((11,)),
            pltpu.SemaphoreType.DMA((11,)),
            pltpu.SemaphoreType.DMA((12,)),
            pltpu.SemaphoreType.DMA((12,)),
            pltpu.SemaphoreType.DMA((2,)),
            pltpu.SemaphoreType.DMA((2,)),
            pltpu.SemaphoreType.DMA((28,)),
            pltpu.SemaphoreType.DMA((28,)),
            pltpu.SemaphoreType.DMA((15,)),
        ],
        compiler_params=pltpu.CompilerParams(
            collective_id=0, has_side_effects=True, vmem_limit_bytes=63 << 20
        ),
        name="conformer_conv",
    )(frames, lengths, ln_gain, w_in, dw_kernel, bn_gain, bn_shift, w_out)


def solution(mesh):
    return jax.shard_map(
        body,
        mesh=mesh,
        in_specs=(
            P("fsdp", "ctx", None),
            P("fsdp"),
            P(),
            P("fsdp", None),
            P(),
            P(),
            P(),
            P("fsdp", None),
        ),
        out_specs=P("fsdp", "ctx", None),
        check_vma=False,
    )
```

time: 83.4 us -> 77.3 us (0.927)
  local copies, waits for them, and re-layouts: 7.34 us -> 2.65 us
  Pallas kernels: 74.6 us -> 73.4 us
    unnamed x9 -> x1, local copies, waits for them, and re-layouts: 5.26 us -> 2.65 us
    reshape x3 -> x0, local copies, waits for them, and re-layouts: 2.08 us -> none  [the longest x1 0.7 us: body(): ln_gain.reshape(1, D)]
    pallas_call x1, Pallas kernels: 74.6 us -> 73.4 us  [body(): pl.pallas_call(kernel, out_shape=jax.ShapeDtypeStruct((1, ROWS, D), BF16)...]
where the time goes in v3:
time: 77.3 us; the launch traced here: 76.7 us
  Pallas kernels  73.4 us (95%)
  local copies, waits for them, and re-layouts  2.65 us (3%)
    pallas_call x1, Pallas kernels, body(): pl.pallas_call(kernel, out_shape=jax.ShapeDtypeStruct((1, ROWS, D), BF16)...  73.4 us
    unnamed x1, local copies, waits for them, and re-layouts  2.65 us

profile of v3, /device:TPU:1, one launch (start us, length us, event | category | flops | bytes accessed | tf_op | source)
XLA Modules:
  0.0 76.7 jit_solution(13689102569696565191)
XLA Ops:
  0.7 73.4 %conformer_conv.1 = bf16[1,512,1536]{2,1,0:T(8,128)(2,1)} custom-call(bf16[1,512,1536]{2,1,0:T(8,128)(2,1)} %frames.1, s32[1]{0:T(128)S(6)} %copy.10.lengths, f32[1536]{0:T(1024)} %ln_gain.1, bf16[64,1536]{1,0:T(8,128)(2,1)} %w_in.1, f32[31,768]{1,0:T(8,128)} %dw.1, f32[768]{0:T(1024)} %bn_gain.1, f32[768]{0:T(1024)} %bn_shift.1, bf16[32,1536]{1,0:T(8,128)(2,1)} %w_out.1), custom_call_target="tpu_custom_call" | custom-call | tf_op jit(solution)/shard_map/conformer_conv/pallas_call | solution.py:446
  74.1 2.7 %copy.11 = bf16[1,512,1536]{2,1,0:T(8,128)(2,1)} copy(bf16[1,512,1536]{2,1,0:T(8,128)(2,1)} %conformer_conv.1) | data formatting | bytes 3145728

commit v4 on v3

--- a/solution.py
+++ b/solution.py
@@ -24,25 +24,22 @@
 
 
 def combine(all_ref, parts):
-    means = [all_ref[i, 0:8, :] for i in range(parts)]
-    counts = [all_ref[i, 6:7, :] for i in range(parts)]
-    squares = [all_ref[i, 8:16, :] for i in range(parts)]
+    tables = [all_ref[i] for i in range(parts)]
+    counts = [all_ref[i, 3:4, :] for i in range(parts)]
     total = sum(counts[1:], counts[0])
-    inverse = 1.0 / jnp.maximum(total, 1.0)
-    weighted = [m * n for m, n in zip(means, counts)]
-    mean = sum(weighted[1:], weighted[0]) * inverse
-    spread = sum(squares[1:], squares[0])
-    for m, n in zip(means, counts):
-        spread = spread + n * (m - mean) * (m - mean)
+    weighted = [m * n for m, n in zip(tables, counts)]
+    mean = sum(weighted[1:], weighted[0]) / jnp.maximum(total, 1.0)
+    added = [n * (m - mean) * (m - mean) for m, n in zip(tables, counts)]
+    square = sum(tables[1:], tables[0]) + pltpu.roll(sum(added[1:], added[0]), 4, 0)
     row = lax.broadcasted_iota(jnp.int32, (8, 128), 0)
-    mean = jnp.where(row == 6, jnp.broadcast_to(total, (8, 128)), mean)
-    return mean, spread
+    rest = jnp.where(row == 7, 0.0, square)
+    return jnp.where(row < 3, mean, jnp.where(row == 3, jnp.broadcast_to(total, (8, 128)), rest))
 
 
 def kernel(
-    frames, lengths, ln_gain, w_in, dw, bn_gain, bn_shift, w_out, out,
-    xbuf, nbuf, wbuf, vbuf, acc, gbuf, cbuf, act, r1, r2, r3, final,
-    gsend, grecv, qsend, qrecv, vsend, vrecv, hsend, hrecv, ssend, srecv, lsem,
+    frames, lengths, ln_gain, w_in, dw, w_out, conv, wide, stats,
+    xbuf, nbuf, wbuf, vbuf, acc, gbuf, cbuf, pay, r1, r2, r3, final,
+    gsend, grecv, qsend, qrecv, vsend, vrecv, hsend, hrecv, ssend, srecv, lsem, csem,
 ):
     f, t = lax.axis_index("fsdp"), lax.axis_index("ctx")
     x, c = (f // 2) % NX, f % 2
@@ -300,10 +297,13 @@
             position = t * ROWS + b + lax.broadcasted_iota(jnp.int32, (BLOCK, 128), 0)
             delta = jnp.where(position < length, cbuf[s, pl.ds(b, BLOCK), :] - mean, 0.0)
             square = square + (delta * delta).reshape(BLOCK // 8, 8, 128).sum(axis=0)
-        r1[slot1, pl.ds(s, 1), :] = mean
-        r1[slot1, pl.ds(s + 8, 1), :] = square.sum(axis=0, keepdims=True)
-
-    r1[slot1] = jnp.zeros((16, 128), F32)
+        pay[s // 3, pl.ds(s % 3, 1), :] = mean
+        pay[s // 3, pl.ds(s % 3 + 4, 1), :] = square.sum(axis=0, keepdims=True)
+        pltpu.make_async_copy(cbuf.at[s], conv.at[s], csem.at[s]).start()
+
+    pay[...] = jnp.zeros((2, 8, 128), F32)
+    for side in (0, 1):
+        pay[side, 3:4, :] = jnp.full((1, 128), local, F32)
 
     X_LAG, Y_LAG, C_LAG = 3, 6, 7
 
@@ -330,9 +330,12 @@
             own_c_send(0)
             own_c_send(1)
 
+        @pl.when(i == 5)
+        def _():
+            v_start()
+
         @pl.when(i == 6)
         def _():
-            v_start()
             own_y_wait()
             own_c_send(2)
 
@@ -349,10 +352,6 @@
         @pl.when(i == 9)
         def _():
             v_x_send()
-
-        @pl.when(i == 12)
-        def _():
-            v_y_send()
 
         @pl.when(i >= C_LAG)
         def _():
@@ -364,51 +363,8 @@
         return carry
 
     lax.fori_loop(0, STRIPS + C_LAG, pipeline, 0)
-    r1[slot1, pl.ds(6, 1), :] = jnp.full((1, 128), local, F32)
-
-    def exchange(ref, slot, count, base, to, between=None):
-        sems = (ssend, srecv)
-        for d in range(1, count):
-            send(ref.at[slot], ref.at[slot], sems, base + d, to(d))
-        if between is not None:
-            between()
-        for d in range(1, count):
-            arrived(ref.at[(slot + count - d) % count], sems, base + d)
-        return combine(ref, count)
-
-    mean, square = exchange(r1, slot1, 8, 0, peer1)
-    r2[y, 0:8, :] = mean
-    r2[y, 8:16, :] = square
-    mean, square = exchange(r2, y, NY, 8, lambda d: at(dy=d))
-    r3[z, 0:8, :] = mean
-    r3[z, 8:16, :] = square
-    mean, square = exchange(r3, z, NZ, 16, lambda d: at(dz=d), v_c_send)
-    count = mean[6:7, :]
-    scale = lax.rsqrt(square / count + 1e-05)
-    v_wait()
-
-    TM = 128
-    final[0:8, :] = mean
-    final[8:16, :] = scale
-
-    def last_step(i, carry):
-        m0 = pl.multiple_of(i * TM, TM)
-        for s in range(STRIPS):
-            lanes = slice(s * 128, (s + 1) * 128)
-            factor = final[8 + s:9 + s, :] * bn_gain[lanes].reshape(1, 128)
-            value = (cbuf[s, pl.ds(m0, TM), :] - final[s:s + 1, :]) * factor + bn_shift[lanes].reshape(1, 128)
-            act[s // 2, :, (s % 2) * 128:(s % 2 + 1) * 128] = (value * sigmoid(value)).astype(BF16)
-        position = t * ROWS + m0 + lax.broadcasted_iota(jnp.int32, (TM, CH), 0)
-        valid = position < length
-        for side in (0, 1):
-            res = 0.0
-            for g in range(3):
-                w = vbuf[g, :, :, side].reshape(256, CH)
-                res = res + jnp.dot(act[(zh + g) % 3], w, preferred_element_type=F32)
-            out[0, pl.ds(m0, TM), side * CH:(side + 1) * CH] = jnp.where(valid, res, 0.0).astype(BF16)
-        return carry
-
-    lax.fori_loop(0, ROWS // TM, last_step, 0)
+    v_y_send()
+
     def drain(j, carry):
         src = wbuf.at[0, x, c, j, :, mine_in]
         for k in (0, 1):
@@ -424,30 +380,94 @@
             remote(ref, ref, gs(j), 7 + part, at(dc=1)).wait_send()
         return carry
 
-    lax.fori_loop(0, STRIPS, drain, 0)
     leaving = [(wbuf.at[0, x, c, direct], qs, k) for k in (0, 1, 2)]
     leaving += [(wbuf.at[0, x, c, split, :, mine_in], qs, k) for k in (3, 4, 5)]
     leaving += [(wbuf.at[0, :, c, split, side, mine_in], qs, 6 + side) for side in (0, 1)]
     leaving += [(own_part(part, c), qs, 8 + part) for part in (0, 1, 2)]
-    leaving += [(vbuf.at[0, x, c, :, mine_out], vs, k) for k in range(5)]
-    leaving += [(vbuf.at[far, x, c, :, mine_out], vs, k) for k in (5, 6, 7)]
-    leaving += [(vbuf.at[:, :, c, side, mine_out], vs, 8 + side) for side in (0, 1)]
-    leaving += [(vbuf.at[:, :, c, :, rows], vs, 10 + k) for k, rows in enumerate((mine_out, other_out))]
-    for ref, sems, k in leaving:
-        remote(ref, ref, sems, k, at(dc=1)).wait_send()
-    for args in sent:
+    later = [(vbuf.at[0, x, c, :, mine_out], vs, k) for k in range(5)]
+    later += [(vbuf.at[far, x, c, :, mine_out], vs, k) for k in (5, 6, 7)]
+    later += [(vbuf.at[:, :, c, side, mine_out], vs, 8 + side) for side in (0, 1)]
+    later += [(vbuf.at[:, :, c, :, rows], vs, 10 + k) for k, rows in enumerate((mine_out, other_out))]
+
+    def settle(items):
+        for ref, sems, k in items:
+            remote(ref, ref, sems, k, at(dc=1)).wait_send()
+
+    def after_z():
+        v_c_send()
+        lax.fori_loop(0, STRIPS, drain, 0)
+        settle(leaving)
+
+    wide_copy = pltpu.make_async_copy(vbuf, wide, csem.at[STRIPS])
+
+    def after_y():
+        v_wait()
+        wide_copy.start()
+        settle(later)
+
+    def exchange(ref, slot, count, base, to, source=None, between=None):
+        sems = (ssend, srecv)
+        for d in range(1, count):
+            src = ref.at[slot] if source is None else source(d)
+            send(src, ref.at[slot], sems, base + d, to(d))
+        if between is not None:
+            between()
+        for d in range(1, count):
+            arrived(ref.at[(slot + count - d) % count], sems, base + d)
+        return combine(ref, count)
+
+    r1[slot1] = pay[c]
+    r2[z] = exchange(r1, slot1, 8, 0, peer1, lambda d: pay.at[(slot1 + d) % 2])
+    r3[y] = exchange(r2, z, NZ, 8, lambda d: at(dz=d), None, after_z)
+    final[c] = exchange(r3, y, NY, 20, lambda d: at(dy=d), None, after_y)
+    send(final.at[c], final.at[c], (ssend, srecv), 0, at(dc=1))
+    for args in sent[:-1]:
         remote(*args).wait_send()
+    for s in range(STRIPS):
+        pltpu.make_async_copy(cbuf.at[s], conv.at[s], csem.at[s]).wait()
+    wide_copy.wait()
+    arrived(final.at[1 - c], (ssend, srecv), 0)
+    stats[...] = final[...]
+    remote(*sent[-1]).wait_send()
+
+
+TM = 128
+
+
+def finish(lengths, stats, bn_gain, bn_shift, conv, wide, out, act):
+    zh, t = lax.axis_index("fsdp") // (2 * NX), lax.axis_index("ctx")
+    for s in range(STRIPS):
+        lanes = slice(s * 128, (s + 1) * 128)
+        side, row = s // 3, s % 3
+        count = stats[side, 3:4, :]
+        spread = stats[side, 4 + row:5 + row, :] / count
+        factor = lax.rsqrt(spread + 1e-05) * bn_gain[lanes].reshape(1, 128)
+        value = (conv[s] - stats[side, row:row + 1, :]) * factor + bn_shift[lanes].reshape(1, 128)
+        act[s // 2, :, (s % 2) * 128:(s % 2 + 1) * 128] = (value * sigmoid(value)).astype(BF16)
+    start = t * ROWS + pl.program_id(0) * TM
+    valid = start + lax.broadcasted_iota(jnp.int32, (TM, CH), 0) < lengths[0]
+    for side in (0, 1):
+        res = 0.0
+        for g in range(3):
+            w = wide[g, :, :, side].reshape(256, CH)
+            res = res + jnp.dot(act[(zh + g) % 3], w, preferred_element_type=F32)
+        out[0, :, side * CH:(side + 1) * CH] = jnp.where(valid, res, 0.0).astype(BF16)
 
 
 def body(frames, lengths, ln_gain, w_in, dw_kernel, bn_gain, bn_shift, w_out):
     hbm = pl.BlockSpec(memory_space=pltpu.HBM)
     vmem = pl.BlockSpec(memory_space=pltpu.VMEM)
     smem = pl.BlockSpec(memory_space=pltpu.SMEM)
-    return pl.pallas_call(
+    wide_shape = (3, NX, 2, 2, 32, CH)
+    conv, wide, stats = pl.pallas_call(
         kernel,
-        out_shape=jax.ShapeDtypeStruct((1, ROWS, D), BF16),
-        in_specs=[hbm, smem, vmem, hbm, vmem, vmem, vmem, hbm],
-        out_specs=vmem,
+        out_shape=(
+            jax.ShapeDtypeStruct((STRIPS, ROWS, 128), F32),
+            jax.ShapeDtypeStruct(wide_shape, BF16),
+            jax.ShapeDtypeStruct((2, 8, 128), F32),
+        ),
+        in_specs=[hbm, smem, vmem, hbm, vmem, hbm],
+        out_specs=(hbm, hbm, vmem),
         scratch_shapes=[
             pltpu.VMEM((ALL, D), BF16),
             pltpu.VMEM((3, ALL, 512), BF16),
@@ -456,11 +476,11 @@
             pltpu.VMEM((6, ALL, 256), F32),
             pltpu.VMEM((STRIPS, ALL, 128), F32),
             pltpu.VMEM((STRIPS, ROWS, 128), F32),
-            pltpu.VMEM((3, 128, 256), BF16),
-            pltpu.VMEM((8, 16, 128), F32),
-            pltpu.VMEM((NY, 16, 128), F32),
-            pltpu.VMEM((NZ, 16, 128), F32),
-            pltpu.VMEM((16, 128), F32),
+            pltpu.VMEM((2, 8, 128), F32),
+            pltpu.VMEM((8, 8, 128), F32),
+            pltpu.VMEM((NZ, 8, 128), F32),
+            pltpu.VMEM((NY, 8, 128), F32),
+            pltpu.VMEM((2, 8, 128), F32),
             pltpu.SemaphoreType.DMA((STRIPS, 9)),
             pltpu.SemaphoreType.DMA((STRIPS, 9)),
             pltpu.SemaphoreType.DMA((11,)),
@@ -472,12 +492,27 @@
             pltpu.SemaphoreType.DMA((28,)),
             pltpu.SemaphoreType.DMA((28,)),
             pltpu.SemaphoreType.DMA((15,)),
+            pltpu.SemaphoreType.DMA((STRIPS + 1,)),
         ],
         compiler_params=pltpu.CompilerParams(
             collective_id=0, has_side_effects=True, vmem_limit_bytes=63 << 20
         ),
         name="conformer_conv",
-    )(frames, lengths, ln_gain, w_in, dw_kernel, bn_gain, bn_shift, w_out)
+    )(frames, lengths, ln_gain, w_in, dw_kernel, w_out)
+    return pl.pallas_call(
+        finish,
+        out_shape=jax.ShapeDtypeStruct((1, ROWS, D), BF16),
+        grid=(ROWS // TM,),
+        in_specs=[
+            smem, vmem, vmem, vmem,
+            pl.BlockSpec((STRIPS, TM, 128), lambda i: (0, i, 0)),
+            pl.BlockSpec(wide_shape, lambda i: (0,) * 6, pipeline_mode=pl.Buffered(1)),
+        ],
+        out_specs=pl.BlockSpec((1, TM, D), lambda i: (0, i, 0)),
+        scratch_shapes=[pltpu.VMEM((3, TM, 256), BF16)],
+        compiler_params=pltpu.CompilerParams(vmem_limit_bytes=63 << 20),
+        name="finish",
+    )(lengths, stats, bn_gain, bn_shift, conv, wide)
 
 
 def solution(mesh):

time: 77.3 us -> 77.1 us (level)
  Pallas kernels: 73.4 us -> 76.2 us
  local copies, waits for them, and re-layouts: 2.65 us -> 0 us
    pallas_call x1 -> x2, Pallas kernels: 73.4 us -> 76.2 us  [the longest x1 70.5 us: body(): pl.pallas_call(kernel, out_shape=(jax.ShapeDtypeStruct((STRIPS, ROWS, 128...]
    unnamed x1 -> x0, local copies, waits for them, and re-layouts: 2.65 us -> none
where the time goes in v4:
time: 77.1 us; the launch traced here: 76.9 us
  Pallas kernels  76.2 us (99%)
    pallas_call x1, Pallas kernels, body(): pl.pallas_call(kernel, out_shape=(jax.ShapeDtypeStruct((STRIPS, ROWS, 128...  70.5 us
    pallas_call x1, Pallas kernels, body(): pl.pallas_call(finish, out_shape=jax.ShapeDtypeStruct((1, ROWS, D), BF16)...  5.66 us

profile of v4, /device:TPU:1, one launch (start us, length us, event | category | flops | bytes accessed | tf_op | source)
XLA Modules:
  0.0 76.9 jit_solution(5205581259034848624)
XLA Ops:
  0.7 70.5 %conformer_conv.1 = (f32[6,512,128]{2,1,0:T(8,128)}, bf16[3,4,2,2,32,768]{5,4,3,2,1,0:T(8,128)(2,1)}, f32[2,8,128]{2,1,0:T(8,128)}) custom-call(bf16[1,512,1536]{2,1,0:T(8,128)(2,1)} %frames.1, s32[1]{0:T(128)S(6)} %copy.9.lengths, f32[1536]{0:T(1024)} %ln_gain.1, bf16[64,1536]{1,0:T(8,128)(2,1)} %w_in.1, f32[31,768]{1,0:T(8,128)} %dw.1, bf16[32,1536]{1,0:T(8,128)(2,1)} %w_out.1), custom_call_target="tpu_custom_call" | custom-call | tf_op jit(solution)/shard_map/conformer_conv/pallas_call | solution.py:462
  71.2 5.7 %finish.1 = bf16[1,512,1536]{2,1,0:T(8,128)(2,1)} custom-call(s32[1]{0:T(128)S(6)} %copy.9.lengths, f32[2,8,128]{2,1,0:T(8,128)} %get-tuple-element.8.stats, f32[768]{0:T(1024)} %bn_gain.1, f32[768]{0:T(1024)} %bn_shift.1, f32[6,512,128]{2,1,0:T(8,128)} %get-tuple-element.9.conv, bf16[3,4,2,2,32,768]{5,4,3,2,1,0:T(8,128)(2,1)} %get-tuple-element.10.wide), custom_call_target="tpu_custom_call" | custom-call | tf_op jit(solution)/shard_map/finish/pallas_call | solution.py:502

commit v5 on v4

--- a/solution.py
+++ b/solution.py
@@ -13,6 +13,7 @@
 ALL = ROWS + 2 * EDGE
 TAPS, CH, D = 31, 768, 1536
 STRIPS = CH // 128
+AHEAD = 4
 
 
 def device_of(x, y, z, c):
@@ -38,7 +39,7 @@
 
 def kernel(
     frames, lengths, ln_gain, w_in, dw, w_out, conv, wide, stats,
-    xbuf, nbuf, wbuf, vbuf, acc, gbuf, cbuf, pay, r1, r2, r3, final,
+    xbuf, nbuf, wbuf, vbuf, gbuf, cbuf, pay, r1, r2, r3, final,
     gsend, grecv, qsend, qrecv, vsend, vrecv, hsend, hrecv, ssend, srecv, lsem, csem,
 ):
     f, t = lax.axis_index("fsdp"), lax.axis_index("ctx")
@@ -225,8 +226,8 @@
 
     for copy in own_in + own_out:
         copy.wait()
-    z_send(0)
-    z_send(1)
+    for j in range(AHEAD):
+        z_send(j)
     xo_send()
     hs = (hsend, hrecv)
     send(frames.at[0, pl.ds(ROWS - EDGE, EDGE)], xbuf.at[pl.ds(0, EDGE)], hs, 0, right)
@@ -258,10 +259,6 @@
         rows = nbuf[(zh + g) % 3, pl.ds(m, size), :]
         return jnp.dot(rows, jnp.concatenate(w, axis=1), preferred_element_type=F32)
 
-    def first_dot(j, carry):
-        acc[j] = dot(0, j, 0, ALL)
-        return carry
-
     length = lengths[0]
     HM = ALL // 2
 
@@ -270,7 +267,7 @@
             m0 = pl.multiple_of(m * HM, 16)
             position = t * ROWS - EDGE + m0 + lax.broadcasted_iota(jnp.int32, (HM, 128), 0)
             valid = (position >= 0) & (position < length)
-            pair = acc[j, pl.ds(m0, HM), :] + (dot(1, j, m0, HM) + dot(2, j, m0, HM))
+            pair = dot(0, j, m0, HM) + dot(1, j, m0, HM) + dot(2, j, m0, HM)
             gated = jnp.where(valid, pair[:, :128] * sigmoid(pair[:, 128:]), 0.0)
             gbuf[j, pl.ds(m0, HM), :] = gated.astype(BF16).astype(F32)
             return carry
@@ -313,9 +310,9 @@
             z_wait(i)
             x_send(i)
 
-        @pl.when(i < STRIPS - 2)
-        def _():
-            z_send(i + 2)
+        @pl.when(i < STRIPS - AHEAD)
+        def _():
+            z_send(jnp.minimum(i + AHEAD, STRIPS - 1))
 
         @pl.when((i >= X_LAG) & (i < STRIPS + X_LAG))
         def _():
@@ -347,7 +344,6 @@
         @pl.when(i == 7)
         def _():
             own_c_wait()
-            lax.fori_loop(0, STRIPS, first_dot, 0)
 
         @pl.when(i == 9)
         def _():
@@ -398,11 +394,14 @@
         lax.fori_loop(0, STRIPS, drain, 0)
         settle(leaving)
 
-    wide_copy = pltpu.make_async_copy(vbuf, wide, csem.at[STRIPS])
+    wide_copies = [
+        pltpu.make_async_copy(vbuf.at[g], wide.at[(zh + g) % 3], csem.at[STRIPS + g]) for g in range(3)
+    ]
 
     def after_y():
         v_wait()
-        wide_copy.start()
+        for copy in wide_copies:
+            copy.start()
         settle(later)
 
     def exchange(ref, slot, count, base, to, source=None, between=None):
@@ -425,17 +424,18 @@
         remote(*args).wait_send()
     for s in range(STRIPS):
         pltpu.make_async_copy(cbuf.at[s], conv.at[s], csem.at[s]).wait()
-    wide_copy.wait()
+    for copy in wide_copies:
+        copy.wait()
     arrived(final.at[1 - c], (ssend, srecv), 0)
     stats[...] = final[...]
     remote(*sent[-1]).wait_send()
 
 
-TM = 128
+TM = 256
 
 
 def finish(lengths, stats, bn_gain, bn_shift, conv, wide, out, act):
-    zh, t = lax.axis_index("fsdp") // (2 * NX), lax.axis_index("ctx")
+    t, i = lax.axis_index("ctx"), pl.program_id(0)
     for s in range(STRIPS):
         lanes = slice(s * 128, (s + 1) * 128)
         side, row = s // 3, s % 3
@@ -443,14 +443,12 @@
         spread = stats[side, 4 + row:5 + row, :] / count
         factor = lax.rsqrt(spread + 1e-05) * bn_gain[lanes].reshape(1, 128)
         value = (conv[s] - stats[side, row:row + 1, :]) * factor + bn_shift[lanes].reshape(1, 128)
-        act[s // 2, :, (s % 2) * 128:(s % 2 + 1) * 128] = (value * sigmoid(value)).astype(BF16)
-    start = t * ROWS + pl.program_id(0) * TM
+        act[:, lanes] = (value * sigmoid(value)).astype(BF16)
+    start = t * ROWS + i * TM
     valid = start + lax.broadcasted_iota(jnp.int32, (TM, CH), 0) < lengths[0]
     for side in (0, 1):
-        res = 0.0
-        for g in range(3):
-            w = wide[g, :, :, side].reshape(256, CH)
-            res = res + jnp.dot(act[(zh + g) % 3], w, preferred_element_type=F32)
+        w = wide[:, :, :, side].reshape(CH, CH)
+        res = jnp.dot(act[...], w, preferred_element_type=F32)
         out[0, :, side * CH:(side + 1) * CH] = jnp.where(valid, res, 0.0).astype(BF16)
 
 
@@ -473,7 +471,6 @@
             pltpu.VMEM((3, ALL, 512), BF16),
             pltpu.VMEM((3, NX, 2, STRIPS, 2, 64, 128), BF16),
             pltpu.VMEM((3, NX, 2, 2, 32, CH), BF16),
-            pltpu.VMEM((6, ALL, 256), F32),
             pltpu.VMEM((STRIPS, ALL, 128), F32),
             pltpu.VMEM((STRIPS, ROWS, 128), F32),
             pltpu.VMEM((2, 8, 128), F32),
@@ -492,7 +489,7 @@
             pltpu.SemaphoreType.DMA((28,)),
             pltpu.SemaphoreType.DMA((28,)),
             pltpu.SemaphoreType.DMA((15,)),
-            pltpu.SemaphoreType.DMA((STRIPS + 1,)),
+            pltpu.SemaphoreType.DMA((STRIPS + 3,)),
         ],
         compiler_params=pltpu.CompilerParams(
             collective_id=0, has_side_effects=True, vmem_limit_bytes=63 << 20
@@ -509,7 +506,7 @@
             pl.BlockSpec(wide_shape, lambda i: (0,) * 6, pipeline_mode=pl.Buffered(1)),
         ],
         out_specs=pl.BlockSpec((1, TM, D), lambda i: (0, i, 0)),
-        scratch_shapes=[pltpu.VMEM((3, TM, 256), BF16)],
+        scratch_shapes=[pltpu.VMEM((TM, CH), BF16)],
         compiler_params=pltpu.CompilerParams(vmem_limit_bytes=63 << 20),
         name="finish",
     )(lengths, stats, bn_gain, bn_shift, conv, wide)

time: 77.1 us -> 74.2 us (0.962)
  Pallas kernels: 76.2 us -> 73.4 us
    pallas_call x1, Pallas kernels: 70.5 us -> 68.7 us  [body(): pl.pallas_call(kernel, out_shape=(jax.ShapeDtypeStruct((STRIPS, ROWS, 128...]
    pallas_call x1, Pallas kernels: 5.66 us -> 4.7 us  [body(): pl.pallas_call(finish, out_shape=jax.ShapeDtypeStruct((1, ROWS, D), BF16)...]
where the time goes in v5:
time: 74.2 us; the launch traced here: 74.1 us
  Pallas kernels  73.4 us (99%)
    pallas_call x1, Pallas kernels, body(): pl.pallas_call(kernel, out_shape=(jax.ShapeDtypeStruct((STRIPS, ROWS, 128...  68.7 us
    pallas_call x1, Pallas kernels, body(): pl.pallas_call(finish, out_shape=jax.ShapeDtypeStruct((1, ROWS, D), BF16)...  4.7 us

profile of v5, /device:TPU:1, one launch (start us, length us, event | category | flops | bytes accessed | tf_op | source)
XLA Modules:
  0.0 74.1 jit_solution(5912197844532125008)
XLA Ops:
  0.7 68.7 %conformer_conv.1 = (f32[6,512,128]{2,1,0:T(8,128)}, bf16[3,4,2,2,32,768]{5,4,3,2,1,0:T(8,128)(2,1)}, f32[2,8,128]{2,1,0:T(8,128)}) custom-call(bf16[1,512,1536]{2,1,0:T(8,128)(2,1)} %frames.1, s32[1]{0:T(128)S(6)} %copy.9.lengths, f32[1536]{0:T(1024)} %ln_gain.1, bf16[64,1536]{1,0:T(8,128)(2,1)} %w_in.1, f32[31,768]{1,0:T(8,128)} %dw.1, bf16[32,1536]{1,0:T(8,128)(2,1)} %w_out.1), custom_call_target="tpu_custom_call" | custom-call | tf_op jit(solution)/shard_map/conformer_conv/pallas_call | solution.py:460
  69.4 4.7 %finish.1 = bf16[1,512,1536]{2,1,0:T(8,128)(2,1)} custom-call(s32[1]{0:T(128)S(6)} %copy.9.lengths, f32[2,8,128]{2,1,0:T(8,128)} %get-tuple-element.8.stats, f32[768]{0:T(1024)} %bn_gain.1, f32[768]{0:T(1024)} %bn_shift.1, f32[6,512,128]{2,1,0:T(8,128)} %get-tuple-element.9.conv, bf16[3,4,2,2,32,768]{5,4,3,2,1,0:T(8,128)(2,1)} %get-tuple-element.10.wide), custom_call_target="tpu_custom_call" | custom-call | tf_op jit(solution)/shard_map/finish/pallas_call | solution.py:499

commit v6 on v5

--- a/solution.py
+++ b/solution.py
@@ -327,7 +327,7 @@
             own_c_send(0)
             own_c_send(1)
 
-        @pl.when(i == 5)
+        @pl.when(i == 4)
         def _():
             v_start()
 
@@ -345,7 +345,7 @@
         def _():
             own_c_wait()
 
-        @pl.when(i == 9)
+        @pl.when(i == 8)
         def _():
             v_x_send()
 

time: 74.2 us -> 73 us (0.984)
  Pallas kernels: 73.4 us -> 72.2 us
    pallas_call x1, Pallas kernels: 68.7 us -> 67.5 us  [body(): pl.pallas_call(kernel, out_shape=(jax.ShapeDtypeStruct((STRIPS, ROWS, 128...]
where the time goes in v6:
time: 73 us; the launch traced here: 72.9 us
  Pallas kernels  72.2 us (99%)
    pallas_call x1, Pallas kernels, body(): pl.pallas_call(kernel, out_shape=(jax.ShapeDtypeStruct((STRIPS, ROWS, 128...  67.5 us
    pallas_call x1, Pallas kernels, body(): pl.pallas_call(finish, out_shape=jax.ShapeDtypeStruct((1, ROWS, D), BF16)...  4.7 us

profile of v6, /device:TPU:1, one launch (start us, length us, event | category | flops | bytes accessed | tf_op | source)
XLA Modules:
  0.0 72.9 jit_solution(9493271418768952243)
XLA Ops:
  0.7 67.5 %conformer_conv.1 = (f32[6,512,128]{2,1,0:T(8,128)}, bf16[3,4,2,2,32,768]{5,4,3,2,1,0:T(8,128)(2,1)}, f32[2,8,128]{2,1,0:T(8,128)}) custom-call(bf16[1,512,1536]{2,1,0:T(8,128)(2,1)} %frames.1, s32[1]{0:T(128)S(6)} %copy.9.lengths, f32[1536]{0:T(1024)} %ln_gain.1, bf16[64,1536]{1,0:T(8,128)(2,1)} %w_in.1, f32[31,768]{1,0:T(8,128)} %dw.1, bf16[32,1536]{1,0:T(8,128)(2,1)} %w_out.1), custom_call_target="tpu_custom_call" | custom-call | tf_op jit(solution)/shard_map/conformer_conv/pallas_call | solution.py:460
  68.2 4.7 %finish.1 = bf16[1,512,1536]{2,1,0:T(8,128)(2,1)} custom-call(s32[1]{0:T(128)S(6)} %copy.9.lengths, f32[2,8,128]{2,1,0:T(8,128)} %get-tuple-element.8.stats, f32[768]{0:T(1024)} %bn_gain.1, f32[768]{0:T(1024)} %bn_shift.1, f32[6,512,128]{2,1,0:T(8,128)} %get-tuple-element.9.conv, bf16[3,4,2,2,32,768]{5,4,3,2,1,0:T(8,128)(2,1)} %get-tuple-element.10.wide), custom_call_target="tpu_custom_call" | custom-call | tf_op jit(solution)/shard_map/finish/pallas_call | solution.py:499
